TPU v7x, 32 devices: a whole 2x2x4 slice. The times are simulated.
32 devices in a mesh: groups: 2 (over x), space: 16 (over z, y, core).
Axes of the slice: x: 2, y: 2, z: 4, core: 2. Of those that a mesh axis runs over, the one named last changes fastest.
Arguments:
- grid_in: bfloat16 [96, 1440, 128], P(('groups', 'space')), parts along dimension 0, may hold values from -6 to 6
- upstream: bfloat16 [96, 1440, 128], P(('groups', 'space')), parts along dimension 0, may hold values from -6 to 6
- mix_weight: bfloat16 [2, 128, 128], replicated, may hold values from -0.375 to 0.375
- degree_filter: bfloat16 [512, 128], replicated, may hold values from 0.25 to 2
Outputs:
- grad_in: bfloat16 [96, 1440, 128], P(('groups', 'space')), parts along dimension 0
- grad_weight: float32 [4, 128, 128], P('groups'), parts along dimension 0
- grad_filter: float32 [1024, 128], P('groups'), parts along dimension 0
There are 2 independent parts, one for each index of `groups`. A program takes and returns all parts, laid end to end along the dimension named above; an argument that names none is the same for every part. Nothing has to cross between parts.
All inputs are finite; a program needn't handle non-finite values.
Results may differ from a plain program's by a relative error of at most 0.02.
Values may be sent and summed in bfloat16 or wider, within the bound.
A program may use at most 128 MiB of HBM per device.

v0:
```python
import math

import jax
import jax.numpy as jnp
from jax import lax
from jax.sharding import PartitionSpec as P

MODES = 512


def latitude_angles(lat_count):
    lat_index = jnp.arange(lat_count, dtype=jnp.float32)
    return math.pi * (lat_index + 0.5) / lat_count


def latitude_weights(lat_count):
    return math.pi / lat_count * jnp.sin(latitude_angles(lat_count))


def legendre_rows(m_values, lat_count, mode_count):
    angles = latitude_angles(lat_count)
    cosine = jnp.cos(angles)[None, :]
    sine_lat = jnp.sin(angles)[None, :]
    orders = m_values.astype(jnp.float32)[:, None]
    log_start = 0.5 * (jnp.log(2.0 * orders + 1.0) - math.log(2.0))
    log_start = log_start + 0.5 * (
        lax.lgamma(2.0 * orders + 1.0) - 2.0 * lax.lgamma(orders + 1.0) - orders * math.log(4.0)
    )
    log_start = log_start + orders * jnp.log(sine_lat)

    def degree_block(carry, block_index):
        p_now, p_prev, log_scale = carry
        outputs = []
        for inner_step in range(32):
            degree = (block_index * 32 + inner_step).astype(jnp.float32)
            active = degree > orders
            denom = jnp.maximum(degree * degree - orders * orders, 1.0)
            coef_a = jnp.sqrt((4.0 * degree * degree - 1.0) / denom)
            lower = jnp.maximum((degree - 1.0) * (degree - 1.0) - orders * orders, 0.0)
            coef_b = jnp.sqrt(
                lower * (2.0 * degree + 1.0) / (jnp.maximum(2.0 * degree - 3.0, 1.0) * denom)
            )
            p_next = jnp.where(active, coef_a * cosine * p_now - coef_b * p_prev, p_now)
            p_prev = jnp.where(active, p_now, p_prev)
            p_now = p_next
            outputs.append(jnp.where(degree >= orders, p_now * jnp.exp(log_scale), 0.0))
        magnitude = jnp.maximum(jnp.abs(p_now), jnp.abs(p_prev))
        next_carry = (p_now / magnitude, p_prev / magnitude, log_scale + jnp.log(magnitude))
        return (next_carry, jnp.stack(outputs, 1))

    ones_grid = jnp.ones((m_values.shape[0], lat_count), jnp.float32)
    start_carry = (ones_grid, jnp.zeros_like(ones_grid), log_start * ones_grid)
    block_ids = jnp.arange(mode_count // 32, dtype=jnp.int32)
    final_carry, stacked = lax.scan(degree_block, start_carry, block_ids)
    return jnp.transpose(stacked, (1, 0, 2, 3)).reshape(m_values.shape[0], mode_count, lat_count)


def fourier_tables(m_order, lon_count):
    lon_index = jnp.arange(lon_count, dtype=jnp.int32)
    phases = m_order[:, None] * lon_index[None, :] % lon_count
    angles = 2.0 * math.pi / lon_count * phases.astype(jnp.float32)
    factor = 1.0 / math.sqrt(lon_count)
    analysis = jnp.stack([jnp.cos(angles) * factor, -jnp.sin(angles) * factor], 1)
    analysis = analysis.reshape(2 * m_order.shape[0], lon_count).astype(jnp.bfloat16)
    doubling = jnp.where(m_order == 0, 1.0, 2.0).astype(jnp.bfloat16)
    synthesis = analysis * jnp.repeat(doubling, 2)[:, None]
    return (analysis, synthesis)


def mixing_matrix(mix_weight):
    upper = jnp.concatenate([mix_weight[0], mix_weight[1]], 1)
    lower = jnp.concatenate([-mix_weight[1], mix_weight[0]], 1)
    return jnp.concatenate([upper, lower], 0)


def fold_weight(block_grad):
    half = block_grad.shape[0] // 2
    real_part = block_grad[:half, :half] + block_grad[half:, half:]
    imag_part = block_grad[:half, half:] - block_grad[half:, :half]
    return jnp.stack([real_part, imag_part], 0)


def gelu_slope(field):
    return 0.5 * (1.0 + lax.erf(field * (1.0 / math.sqrt(2.0)))) + field * jnp.exp(
        -0.5 * field * field
    ) * (1.0 / math.sqrt(2.0 * math.pi))


def body(grid_in, upstream, mix_weight, degree_filter):
    devices = lax.axis_size("space")
    device_index = lax.axis_index("space")
    lat_local, lon_count, channels = grid_in.shape
    lat_count = lat_local * devices
    per_device = MODES // devices
    positions = jnp.arange(MODES, dtype=jnp.int32)
    slot_index = jnp.arange(per_device, dtype=jnp.int32)
    m_order = positions % per_device * devices + positions // per_device
    slot_orders = slot_index * devices + device_index
    quarter = per_device // 4
    sections = [
        (part_id * quarter, (part_id + 1) * quarter, part_id * (MODES // 4)) for part_id in range(4)
    ]
    analysis, synthesis = fourier_tables(m_order, lon_count)
    legendre = legendre_rows(slot_orders, lat_count, MODES)
    synth_table = legendre.astype(jnp.bfloat16)
    anal_table = (legendre * latitude_weights(lat_count)).astype(jnp.bfloat16)
    wide_weight = mixing_matrix(mix_weight)
    filter_gain = degree_filter.astype(jnp.float32)
    fourier = jnp.einsum("kn,anc->akc", analysis, grid_in, preferred_element_type=jnp.float32)
    fourier = fourier.astype(jnp.bfloat16).reshape(lat_local, MODES, 2 * channels)
    spectral_in = lax.all_to_all(fourier, "space", split_axis=1, concat_axis=0, tiled=True)
    saved = []
    pieces = []
    for start_slot, stop_slot, first_degree in sections:
        spectrum = jnp.einsum(
            "jla,ajx->jlx",
            anal_table[start_slot:stop_slot, first_degree:],
            spectral_in[:, start_slot:stop_slot],
            preferred_element_type=jnp.float32,
        ).astype(jnp.bfloat16)
        slot_count, degree_count = (spectrum.shape[0], spectrum.shape[1])
        spectrum = spectrum.reshape(slot_count, degree_count, 2, channels)
        scaled = (
            spectrum.astype(jnp.float32) * filter_gain[first_degree:][None, :, None, :]
        ).astype(jnp.bfloat16)
        scaled_rows = scaled.reshape(slot_count * degree_count, 2 * channels)
        mixed = jnp.dot(scaled_rows, wide_weight, preferred_element_type=jnp.float32).astype(
            jnp.bfloat16
        )
        mixed = mixed.reshape(slot_count, degree_count, 2 * channels)
        pieces.append(
            jnp.einsum(
                "jla,jlx->ajx",
                synth_table[start_slot:stop_slot, first_degree:],
                mixed,
                preferred_element_type=jnp.float32,
            ).astype(jnp.bfloat16)
        )
        saved.append((spectrum, scaled_rows))
    grid_modes = jnp.concatenate(pieces, 1)
    returned = lax.all_to_all(grid_modes, "space", split_axis=0, concat_axis=1, tiled=True)
    field = jnp.einsum(
        "kn,akc->anc",
        synthesis,
        returned.reshape(lat_local, 2 * MODES, channels),
        preferred_element_type=jnp.float32,
    )
    slope = (upstream.astype(jnp.float32) * gelu_slope(field)).astype(jnp.bfloat16)
    gfourier = jnp.einsum("kn,anc->akc", synthesis, slope, preferred_element_type=jnp.float32)
    gfourier = gfourier.astype(jnp.bfloat16).reshape(lat_local, MODES, 2 * channels)
    gradient_in = lax.all_to_all(gfourier, "space", split_axis=1, concat_axis=0, tiled=True)
    weight_total = jnp.zeros((2 * channels, 2 * channels), jnp.float32)
    filter_total = jnp.zeros((MODES, channels), jnp.float32)
    gpieces = []
    for (start_slot, stop_slot, first_degree), (spectrum, scaled_rows) in zip(sections, saved):
        gmixed = jnp.einsum(
            "jla,ajx->jlx",
            synth_table[start_slot:stop_slot, first_degree:],
            gradient_in[:, start_slot:stop_slot],
            preferred_element_type=jnp.float32,
        ).astype(jnp.bfloat16)
        slot_count, degree_count = (gmixed.shape[0], gmixed.shape[1])
        gmixed_rows = gmixed.reshape(slot_count * degree_count, 2 * channels)
        weight_total = weight_total + lax.dot_general(
            scaled_rows, gmixed_rows, (((0,), (0,)), ((), ())), preferred_element_type=jnp.float32
        )
        gscaled = lax.dot_general(
            gmixed_rows, wide_weight, (((1,), (1,)), ((), ())), preferred_element_type=jnp.float32
        )
        gscaled = gscaled.reshape(slot_count, degree_count, 2, channels)
        filter_part = jnp.sum(gscaled * spectrum.astype(jnp.float32), axis=(0, 2))
        filter_total = filter_total + jnp.pad(filter_part, ((first_degree, 0), (0, 0)))
        gspectrum = (gscaled * filter_gain[first_degree:][None, :, None, :]).astype(jnp.bfloat16)
        gspectrum = gspectrum.reshape(slot_count, degree_count, 2 * channels)
        gpieces.append(
            jnp.einsum(
                "jla,jlx->ajx",
                anal_table[start_slot:stop_slot, first_degree:],
                gspectrum,
                preferred_element_type=jnp.float32,
            ).astype(jnp.bfloat16)
        )
    gfield_modes = jnp.concatenate(gpieces, 1)
    gfield = lax.all_to_all(gfield_modes, "space", split_axis=0, concat_axis=1, tiled=True)
    grad_in = jnp.einsum(
        "kn,akc->anc",
        analysis,
        gfield.reshape(lat_local, 2 * MODES, channels),
        preferred_element_type=jnp.float32,
    )
    grad_in = (grad_in + upstream.astype(jnp.float32)).astype(jnp.bfloat16)
    summed, grad_filter = lax.psum((weight_total * (1.0 / MODES), filter_total * 0.125), "space")
    grad_weight = fold_weight(summed)
    return (grad_in, grad_weight, grad_filter)


def solution(mesh):
    return jax.shard_map(
        body,
        mesh=mesh,
        in_specs=(P(("groups", "space"), None, None), P(("groups", "space"), None, None), P(), P()),
        out_specs=(P(("groups", "space"), None, None), P("groups", None, None), P("groups", None)),
        check_vma=False,
    )
```

profile of v0, /device:TPU:0, one launch (start us, length us, event | category | flops | bytes accessed | tf_op | source)
XLA Modules:
  0.0 464.4 jit_solution(1075074810099635511)
XLA Ops:
  7.2 12.8 %cosine_multiply_fusion = (bf16[512,1,1440]{0,2,1:T(8,128)(2,1)S(1)}, bf16[512,1,1440]{0,2,1:T(8,128)(2,1)S(1)}) fusion(s32[512]{0:T(512)S(1)} %fusion.108), kind=kLoop, calls=%fused_computation.328 | loop fusion | flops 10321920 | bytes 2951168 | tf_op jit(solution)/shard_map/mul | solution.py:63
  20.0 2.9 broadcast_multiply_fusion
  22.9 8.8 %copy.176 = bf16[512,2,1440]{2,1,0:T(2,128)(2,1)} copy(bf16[512,2,1440]{0,2,1:T(8,128)(2,1)} %get-tuple-element.620) | data formatting | bytes 5898240 | tf_op jit(solution)/shard_map/convert_element_type | solution.py:64
  31.8 7.5 %convert_element_type.660 = bf16[1024,1440]{1,0:T(8,128)(2,1)} reshape(bf16[512,2,1440]{2,1,0:T(2,128)(2,1)} %copy.176) | data formatting | bytes 5898240 | tf_op jit(solution)/shard_map/convert_element_type | solution.py:64
  39.3 3.7 fusion.54
  43.2 1.6 copy.178
  44.9 8.0 %all-to-all-start = ((bf16[3,512,256]{2,0,1:T(4,128)(2,1)}), bf16[3,512,256]{2,0,1:T(4,128)(2,1)}, u32[]{:S(2)}, u32[]{:S(2)}) async-start(bf16[3,512,256]{2,0,1:T(4,128)(2,1)} %copy.178), calls=%async_computation | async-start | bytes 2097152 | tf_op jit(solution)/shard_map/all_to_all | solution.py:111
  53.1 118.9 %while.23 = (s32[]{:T(128)}, f32[32,48]{1,0:T(8,128)S(1)}, f32[32,48]{1,0:T(8,128)S(1)}, f32[32,48]{1,0:T(8,128)S(1)}, f32[16,32,32,48]{3,1,2,0:T(8,128)}, /*ind...) while((s32[]{:T(128)}, f32[32,48]{1,0:T(8,128)S(1)}, ...), condition=%wide.region_1.2_spmd.clone.clone.clone.clone, body=%wide.region_0.1_spmd.clone.clone.clone.clone.sunk | while | flops 476130 | bytes 4452125 | solution.py:54
  174.1 5.2 %copy.242 = f32[32,512,48]{1,2,0:T(8,128)S(1)} copy(f32[32,512,48]{2,0,1:T(8,128)} %bitcast.851) | data formatting | bytes 6291456 | tf_op jit(solution)/shard_map/reshape | solution.py:55
  179.8 5.8 %copy.267 = f32[32,8,8,512]{3,1,2,0:T(8,128)} copy(f32[32,8,8,512]{3,2,1,0:T(8,128)S(1)} %bitcast.843) | data formatting | bytes 8388608
  185.7 1.7 copy.260
  187.4 1.1 mul.4632.clone
  188.5 2.2 copy.268
  191.9 2.2 copy.269
  194.1 1.6 copy.262
  197.3 2.3 fusion.127
  199.6 1.5 copy.179
  202.0 2.8 convert_convert_fusion
  204.7 5.7 %copy.184 = f32[4096,256]{0,1:T(8,128)} copy(f32[4096,256]{1,0:T(8,128)} %bitcast.841) | data formatting | bytes 8388608 | tf_op jit(solution)/shard_map/convert_element_type | solution.py:124
  210.5 1.6 fusion.43
  212.1 2.4 copy.188
  214.5 5.0 %convolution_convert_fusion = bf16[4096,256]{1,0:T(8,128)(2,1)S(1)} fusion(f32[4096,256]{0,1:T(8,128)} %copy.184, f32[4096,256]{0,1:T(8,128)} %bitcast.842, bf16[128,128]{1,0:T(8,128)(2,1)S(1)} %get-tuple-element.776, bf16[128,128]{1,0:T(8,128)(2,1)S(1)} %fusion.126, bf16[128,128]{1,0:T(8,128)(2,1)S(1)} %get-tuple-element.775), kind=kOutput, calls=%fused_computation.300 | convolution fusion | flops 540540928 | bytes 10584064 | tf_op jit(solution)/shard_map/dot_general | solution.py:127
  219.5 2.1 fusion.64
  222.7 2.1 fusion.69
  224.8 2.8 fusion.47
  227.5 2.9 copy.192
  230.5 3.0 convolution_convert_fusion.2
  233.5 1.9 fusion.67
  235.4 2.2 fusion.60
  237.6 2.5 copy.196
  241.2 1.7 convolution_convert_fusion.8
  245.3 6.4 %all-to-all-start.1 = ((bf16[48,32,256]{2,1,0:T(8,128)(2,1)}), bf16[48,32,256]{2,1,0:T(8,128)(2,1)}, u32[]{:S(2)}, u32[]{:S(2)}) async-start(bf16[48,32,256]{2,1,0:T(8,128)(2,1)} %copy.197), calls=%async_computation.1 | async-start | bytes 1572864 | tf_op jit(solution)/shard_map/all_to_all | solution.py:141
  251.6 8.8 %copy.199 = bf16[512,2,1440]{2,1,0:T(2,128)(2,1)} copy(bf16[512,2,1440]{0,2,1:T(8,128)(2,1)} %get-tuple-element.619) | data formatting | bytes 5898240 | tf_op jit(solution)/shard_map/mul | solution.py:66
  260.5 7.5 %mul.4643 = bf16[1024,1440]{1,0:T(8,128)(2,1)} reshape(bf16[512,2,1440]{2,1,0:T(2,128)(2,1)} %copy.199) | data formatting | bytes 5898240 | tf_op jit(solution)/shard_map/mul | solution.py:66
  268.3 2.1 all-to-all-done.1
  270.4 2.1 copy.198
  272.4 2.1 reshape.2792
  274.5 8.0 %fusion.57 = bf16[3,1024,128]{1,2,0:T(8,128)(2,1)} fusion(bf16[1024,1440]{1,0:T(8,128)(2,1)} %convert_element_type.660, bf16[1024]{0:T(1024)(128)(2,1)S(1)} %mul.4655, bf16[3,1440,128]{2,1,0:T(8,128)(2,1)} %param.7, bf16[3,1024,128]{2,1,0:T(8,128)(2,1)} %reshape.2792, bf16[1024,1440]{1,0:T(8,128)(2,1)} %mul.4643), kind=kOutput, calls=%fused_computation.363 | convolution fusion | flops 2272874496 | bytes 8579072 | tf_op jit(solution)/shard_map/kn,anc->akc/dot_general | solution.py:149
  282.5 2.3 copy.202
  284.8 2.1 reshape.2793
  286.9 2.8 copy.203
  289.7 5.4 %all-to-all-start.2 = ((bf16[3,512,256]{2,0,1:T(4,128)(2,1)}), bf16[3,512,256]{2,0,1:T(4,128)(2,1)}, u32[]{:S(2)}, u32[]{:S(2)}) async-start(bf16[3,512,256]{2,0,1:T(4,128)(2,1)} %copy.203), calls=%async_computation.2 | async-start | bytes 2097152 | tf_op jit(solution)/shard_map/all_to_all | solution.py:151
  296.0 5.3 %copy.247 = f32[8,512,256]{1,2,0:T(8,128)} copy(f32[8,512,256]{2,1,0:T(8,128)} %convert_convert_fusion) | data formatting | bytes 8388608 | tf_op jit(solution)/shard_map/convert_element_type | solution.py:124
  301.3 2.4 copy.248
  303.7 2.3 copy.249
  306.0 1.3 copy.250
  307.3 10.8 %all-to-all-done.2 = bf16[3,512,256]{2,0,1:T(4,128)(2,1)} async-done(((bf16[3,512,256]{2,0,1:T(4,128)(2,1)}), bf16[3,512,256]{2,0,1:T(4,128)(2,1)}, u32[]{:S(2)}, u32[]{:S(2)}) %all-to-all-start.2) | async-done | bytes 786464 | tf_op jit(solution)/shard_map/all_to_all | solution.py:151
  318.1 1.5 copy.204
  322.1 2.2 copy-done.2
  324.3 2.2 multiply_reduce_fusion
  326.5 1.2 copy.218
  327.6 2.2 copy.271
  329.9 1.3 multiply_reduce_fusion.1
  332.1 1.5 copy.272
  333.6 1.3 multiply_reduce_fusion.2
  335.5 1.3 copy.273
  337.2 1.2 copy.224
  340.5 1.1 copy.214
  341.7 6.8 %all-to-all-start.3 = ((bf16[48,32,256]{2,1,0:T(8,128)(2,1)}), bf16[48,32,256]{2,1,0:T(8,128)(2,1)}, u32[]{:S(2)}, u32[]{:S(2)}) async-start(bf16[48,32,256]{2,1,0:T(8,128)(2,1)} %copy.214), calls=%async_computation.3 | async-start | bytes 1572864 | tf_op jit(solution)/shard_map/all_to_all | solution.py:184
  348.9 2.4 fusion.130
  355.0 92.3 %all-reduce.6.cloned.1.call-done = (f32[256,256]{1,0:T(8,128)}, f32[512,128]{0,1:T(8,128)}) async-done(((f32[256,256]{1,0:T(8,128)}, f32[512,128]{0,1:T(8,128)}), (f32[256,256]{1,0:T(8,128)}, f32[512,128]{0,1:T(8,128)})) %all-reduce.6.cloned.1.call-update) | async-done | bytes 524304 | tf_op jit(solution)/shard_map/psum | solution.py:192
  447.3 1.9 copy.229
  450.8 1.2 copy.215
  452.3 4.8 %fusion.31 = bf16[3,1440,128]{2,1,0:T(8,128)(2,1)} fusion(bf16[3,1024,128]{2,1,0:T(8,128)(2,1)S(1)} %reshape.2798, bf16[1024,1440]{1,0:T(8,128)(2,1)} %convert_element_type.660, bf16[3,1440,128]{2,1,0:T(8,128)(2,1)S(1)} %copy-done.35), kind=kOutput, calls=%fused_computation.333 | convolution fusion | flops 1134120960 | bytes 5947392 | tf_op jit(solution)/shard_map/kn,akc->anc/dot_general | solution.py:185
  (1743 shorter events, 114.0 us)
Async XLA Ops:
  7.2 32.1 %copy-start = (bf16[3,1440,128]{2,1,0:T(8,128)(2,1)S(1)}, bf16[3,1440,128]{2,1,0:T(8,128)(2,1)}, u32[]{:S(2)}) copy-start(bf16[3,1440,128]{2,1,0:T(8,128)(2,1)} %param.6) | copy-start | bytes 3317764
  44.9 154.7 %all-to-all-start = ((bf16[3,512,256]{2,0,1:T(4,128)(2,1)}), bf16[3,512,256]{2,0,1:T(4,128)(2,1)}, u32[]{:S(2)}, u32[]{:S(2)}) async-start(bf16[3,512,256]{2,0,1:T(4,128)(2,1)} %copy.178), calls=%async_computation | async-start | bytes 2097152 | tf_op jit(solution)/shard_map/all_to_all | solution.py:111
  53.1 118.9 %copy-start.20 = (bf16[512,128]{1,0:T(8,128)(2,1)S(1)}, bf16[512,128]{1,0:T(8,128)(2,1)}, u32[]{:S(2)}) copy-start(bf16[512,128]{1,0:T(8,128)(2,1)} %param.9) | copy-start | bytes 393220
  191.7 2.3 copy-start.25
  196.5 44.7 %copy-start.22 = (bf16[128,128]{1,0:T(8,128)(2,1)}, bf16[128,128]{1,0:T(8,128)(2,1)S(1)}, u32[]{:S(2)}) copy-start(bf16[128,128]{1,0:T(8,128)(2,1)S(1)} %fusion.126) | copy-start | bytes 98308
  197.2 43.9 %copy-start.23 = (bf16[128,128]{1,0:T(8,128)(2,1)}, bf16[128,128]{1,0:T(8,128)(2,1)S(1)}, u32[]{:S(2)}) copy-start(bf16[128,128]{1,0:T(8,128)(2,1)S(1)} %get-tuple-element.775) | copy-start | bytes 98308
  197.3 43.9 %copy-start.24 = (bf16[128,128]{1,0:T(8,128)(2,1)}, bf16[128,128]{1,0:T(8,128)(2,1)S(1)}, u32[]{:S(2)}) copy-start(bf16[128,128]{1,0:T(8,128)(2,1)S(1)} %get-tuple-element.776) | copy-start | bytes 98308
  199.6 2.4 copy-start.13
  214.5 7.1 %copy-start.6 = (f32[32,8,8,384]{3,1,2,0:T(8,128)S(1)}, f32[32,8,8,384]{3,1,2,0:T(8,128)}, u32[]{:S(2)}) copy-start(f32[32,8,8,384]{3,1,2,0:T(8,128)} %copy.268) | copy-start | bytes 9437188
  214.5 7.1 %copy-start.7 = (f32[3072,256]{0,1:T(8,128)S(1)}, f32[3072,256]{0,1:T(8,128)}, u32[]{:S(2)}) copy-start(f32[3072,256]{0,1:T(8,128)} %copy.188) | copy-start | bytes 9437188
  222.7 2.1 copy-start.28
  230.5 4.9 %copy-start.29 = (bf16[48,8,256]{2,1,0:T(8,128)(2,1)S(1)}, bf16[48,8,256]{2,1,0:T(8,128)(2,1)}, u32[]{:S(2)}) copy-start(bf16[48,8,256]{2,1,0:T(8,128)(2,1)} %get-tuple-element.768) | copy-start | bytes 589828
  240.1 3.9 copy-start.30
  240.1 3.9 copy-start.31
  240.2 3.9 copy-start.32
  245.3 25.1 %all-to-all-start.1 = ((bf16[48,32,256]{2,1,0:T(8,128)(2,1)}), bf16[48,32,256]{2,1,0:T(8,128)(2,1)}, u32[]{:S(2)}, u32[]{:S(2)}) async-start(bf16[48,32,256]{2,1,0:T(8,128)(2,1)} %copy.197), calls=%async_computation.1 | async-start | bytes 1572864 | tf_op jit(solution)/shard_map/all_to_all | solution.py:141
  289.7 28.4 %all-to-all-start.2 = ((bf16[3,512,256]{2,0,1:T(4,128)(2,1)}), bf16[3,512,256]{2,0,1:T(4,128)(2,1)}, u32[]{:S(2)}, u32[]{:S(2)}) async-start(bf16[3,512,256]{2,0,1:T(4,128)(2,1)} %copy.203), calls=%async_computation.2 | async-start | bytes 2097152 | tf_op jit(solution)/shard_map/all_to_all | solution.py:151
  303.7 2.3 copy-start.8
  318.1 1.7 copy-start.15
  320.6 1.5 copy-start.11
  320.6 3.7 copy-start.2
  321.2 8.7 %copy-start.4 = (bf16[8,384,256]{2,1,0:T(8,128)(2,1)}, bf16[8,384,256]{2,1,0:T(8,128)(2,1)S(1)}, u32[]{:S(2)}) copy-start(bf16[8,384,256]{2,1,0:T(8,128)(2,1)S(1)} %convolution_convert_fusion.4) | copy-start | bytes 4718596
  322.0 14.7 %copy-start.16 = (bf16[8,128,256]{2,1,0:T(8,128)(2,1)}, bf16[8,128,256]{2,1,0:T(8,128)(2,1)S(1)}, u32[]{:S(2)}) copy-start(bf16[8,128,256]{2,1,0:T(8,128)(2,1)S(1)} %convolution_convert_fusion.9) | copy-start | bytes 1572868
  327.6 2.3 copy-start.3
  327.6 2.3 copy-start.21
  332.1 1.5 copy-start.26
  334.9 1.9 copy-start.9
  334.9 1.9 copy-start.33
  336.8 1.6 copy-start.14
  340.4 8.4 %copy-start.10 = (bf16[32,8,8,512]{3,1,2,0:T(8,128)(2,1)S(1)}, bf16[32,8,8,512]{3,1,2,0:T(8,128)(2,1)}, u32[]{:S(2)}) copy-start(bf16[32,8,8,512]{3,1,2,0:T(8,128)(2,1)} %copy.271) | copy-start | bytes 6291460
  341.7 109.1 %all-to-all-start.3 = ((bf16[48,32,256]{2,1,0:T(8,128)(2,1)}), bf16[48,32,256]{2,1,0:T(8,128)(2,1)}, u32[]{:S(2)}, u32[]{:S(2)}) async-start(bf16[48,32,256]{2,1,0:T(8,128)(2,1)} %copy.214), calls=%async_computation.3 | async-start | bytes 1572864 | tf_op jit(solution)/shard_map/all_to_all | solution.py:184
  348.5 98.8 %all-reduce.6.cloned.1.call-start = ((), (), s32[]{:S(2)}) async-start(), calls=%async_computation.4 | async-start | bytes 1048576 | tf_op jit(solution)/shard_map/psum | solution.py:192
  348.9 2.5 copy-start.27
  348.9 2.5 copy-start.34
  348.9 3.3 copy-start.5
  348.9 3.3 copy-start.12
  351.4 1.4 copy-start.18
  352.7 1.0 copy-start.17
  352.7 1.2 copy-start.19
  447.3 5.0 %copy-start.35 = (bf16[3,1440,128]{2,1,0:T(8,128)(2,1)S(1)}, bf16[3,1440,128]{2,1,0:T(8,128)(2,1)}, u32[]{:S(2)}) copy-start(bf16[3,1440,128]{2,1,0:T(8,128)(2,1)} %param.7) | copy-start | bytes 3317764
  452.3 4.8 %copy-start.1 = (bf16[3,1440,128]{2,1,0:T(8,128)(2,1)S(1)}, bf16[3,1440,128]{2,1,0:T(8,128)(2,1)}, u32[]{:S(2)}) copy-start(bf16[3,1440,128]{2,1,0:T(8,128)(2,1)} %param.6) | copy-start | bytes 3317764
Sparse Core Ops, SparseCore 0:
  355.1 92.1 all-reduce.5
where the time goes:
time: 472 us; the launch traced here: 464 us
  local copies, waits for them, and re-layouts  142 us (30%)
  waiting for transfers between devices  105 us (22%)
  other arithmetic  87.9 us (19%)
  matrix products  57.6 us (12%)
  loops' own time  29.5 us (6%)
  starting transfers between devices  27 us (6%)
  between operations  15.2 us (3%)
    psum x1, waiting for transfers between devices, body(): lax.psum((weight_total * (1.0 / MODES), filter_total * 0.125), 'space')  92.3 us
    while x496, other arithmetic  46.5 us
    another operation x1, loops' own time, legendre_rows(): final_carry, stacked = lax.scan(degree_block, start_carry, block_ids)  29.5 us
    convert_element_type x8, local copies, waits for them, and re-layouts, body(): spectrum.astype(jnp.float32) * filter_gain[first_degree:][None, :, None, :]  24.9 us
    unnamed x83, local copies, waits for them, and re-layouts  24.7 us
    mul x3, local copies, waits for them, and re-layouts, fourier_tables(): synthesis = analysis * jnp.repeat(doubling, 2)[:, None]  16.5 us
    convert_element_type x2, local copies, waits for them, and re-layouts, fourier_tables(): analysis.reshape(2 * m_order.shape[0], lon_count).astype(jnp.bfloat16)  16.4 us
    dynamic_update_slice x16, local copies, waits for them, and re-layouts, legendre_rows(): final_carry, stacked = lax.scan(degree_block, start_carry, block_ids)  13.6 us
  transfers between devices with their start and end apart: 5, of which 3 were waited for; matrix products, arithmetic and copies ran while one was open for 33% of the time, Pallas kernels for 0%

commit v1 on v0

v1 whole, which is shorter than its diff:
```python
import functools
import math

import jax
import jax.numpy as jnp
from jax import lax
from jax.experimental import pallas as pl
from jax.experimental.pallas import tpu as pltpu
from jax.sharding import PartitionSpec as P

MODES = 512
ROWS = 32
F32 = jnp.float32
BF16 = jnp.bfloat16


def params(**extra):
    return pltpu.CompilerParams(vmem_limit_bytes=56 * 1024 * 1024, **extra)


def latitude_angles(index, lat_count):
    return math.pi * (index.astype(F32) + 0.5) / lat_count


def row_phase(rows, devices, lon_count):
    slots = MODES // devices
    device = rows // (2 * slots)
    part = rows // slots % 2
    order = rows % slots * devices + device
    return order, part * (lon_count // 4)


def trig(phases, lon_count):
    angles = 2.0 * math.pi / lon_count * (phases % lon_count).astype(F32)
    return jnp.stack([jnp.cos(angles), jnp.sin(angles)], 0)


def base_tables(devices, lon_count):
    total = 2 * MODES
    lon = jnp.arange(lon_count, dtype=jnp.int32)
    factor = 1.0 / math.sqrt(lon_count)
    order, offset = row_phase(jnp.arange(total, dtype=jnp.int32), devices, lon_count)
    fine = order[:ROWS, None] * lon[None, :] + offset[:ROWS, None]
    coarse = order[::ROWS, None] * lon[None, :] + offset[::ROWS, None]
    tfine = lon[:ROWS, None] * order[None, :] + offset[None, :]
    tcoarse = lon[::ROWS, None] * order[None, :]
    return (
        trig(coarse, lon_count),
        trig(fine, lon_count) * factor,
        trig(tcoarse, lon_count),
        trig(tfine, lon_count) * factor,
    )


def fourier_kernel(coarse, fine, tcoarse, tfine, grid, table, ttable, out):
    lat_local = grid.shape[0]
    devices, span = out.shape[0], out.shape[1]

    def fill(dst, big, small):
        def step(h, carry):
            value = big[0, pl.ds(h, 1), :] * small[0] - big[1, pl.ds(h, 1), :] * small[1]
            dst[pl.ds(pl.multiple_of(h * ROWS, ROWS), ROWS), :] = value.astype(BF16)
            return carry

        lax.fori_loop(0, big.shape[1], step, 0)

    fill(table, coarse, fine)
    fill(ttable, tcoarse, tfine)
    wide = jnp.concatenate([grid[a] for a in range(lat_local)], 1)
    chunk = 256

    def product(q, carry):
        rows = pl.ds(pl.multiple_of(q * chunk, chunk), chunk)
        value = jnp.dot(table[rows, :], wide, preferred_element_type=F32)
        value = value.astype(BF16).reshape(chunk // span, span, value.shape[1])
        out[pl.ds(q * (chunk // span), chunk // span)] = value
        return carry

    lax.fori_loop(0, 2 * MODES // chunk, product, 0)


def legendre_kernel(order_ref, cos_ref, start_ref, weight_ref, wcol_ref, synth, anal, tsynth, tanal, hold):
    groups, width = order_ref.shape
    orders = order_ref[...]
    order_sq = orders * orders
    cosine = cos_ref[...]
    weight = weight_ref[...]
    block = 32

    def degree_block(index, carry):
        p_now, p_prev, e_prev, log_scale = carry
        scale = jnp.exp(log_scale)
        base = index * block
        for inner in range(block):
            degree_int = base + inner
            degree = degree_int.astype(F32)
            active = degree > orders
            square = degree * degree
            ratio = jnp.maximum(square - order_sq, 1.0) / jnp.maximum(4.0 * square - 1.0, 1.0)
            coef = lax.rsqrt(ratio)
            p_next = jnp.where(active, coef * (cosine * p_now - e_prev * p_prev), p_now)
            p_prev = jnp.where(active, p_now, p_prev)
            e_prev = jnp.where(active, ratio * coef, 0.0)
            p_now = p_next
            value = jnp.where(degree >= orders, p_now * scale, 0.0)
            rows = pl.ds(pl.multiple_of(degree_int * groups, groups), groups)
            for part in range(width // 128):
                hold[part, rows, :] = value[:, part * 128 : (part + 1) * 128]
        magnitude = jnp.maximum(jnp.abs(p_now), jnp.abs(p_prev))
        return (p_now / magnitude, p_prev / magnitude, e_prev, log_scale + jnp.log(magnitude))

    ones = jnp.ones((groups, width), F32)
    zeros = jnp.zeros((groups, width), F32)
    lax.fori_loop(0, MODES // block, degree_block, (ones, zeros, zeros, start_ref[...]))

    def spread(g, carry):
        wrow = weight[0:1, :]
        pieces = [
            hold[part, pl.ds(g, MODES, stride=groups), :]
            for part in range(width // 128)
        ]
        value = pieces[0] if len(pieces) == 1 else jnp.concatenate(pieces, 1)
        synth[g] = value.astype(BF16)
        anal[g] = (value * wrow).astype(BF16)
        turned = value.T
        tsynth[g] = turned.astype(BF16)
        tanal[g] = (turned * wcol_ref[:, 0:1]).astype(BF16)
        return carry

    lax.fori_loop(0, synth.shape[0], spread, 0)


def unpack(src, scratch):
    devices, span, _ = src.shape
    for a in range(scratch.shape[0]):
        part = src[:, :, a * 128 : (a + 1) * 128].astype(F32)
        scratch[a] = part.reshape(devices * span, 128)


def pack(scratch, dst):
    devices, span, _ = dst.shape
    for a in range(scratch.shape[0]):
        dst[:, :, a * 128 : (a + 1) * 128] = (
            scratch[a].reshape(devices, span, 128).astype(BF16)
        )


def gather_group(scratch, g, devices, span, per_group, height):
    lat_local = scratch.shape[0]
    slots = span // 2
    rows = []
    for j in range(per_group):
        s = g * per_group + j
        halves = []
        for r in range(2):
            parts = [
                scratch[a, pl.ds(r * slots + s, devices, stride=span), :] for a in range(lat_local)
            ]
            if height > devices * lat_local:
                parts.append(jnp.zeros((height - devices * lat_local, 128), F32))
            halves.append(jnp.concatenate(parts, 0))
        zero = jnp.zeros((height, 256), F32)
        cells = [zero] * per_group
        cells[j] = jnp.concatenate(halves, 1)
        rows.append(cells[0] if per_group == 1 else jnp.concatenate(cells, 1))
    return (rows[0] if per_group == 1 else jnp.concatenate(rows, 0)).astype(BF16)


def scatter_group(value, scratch, g, devices, span, per_group, height):
    lat_local = scratch.shape[0]
    slots = span // 2
    for j in range(per_group):
        s = g * per_group + j
        for r in range(2):
            for a in range(lat_local):
                top = j * height + a * devices
                left = j * 256 + r * 128
                scratch[a, pl.ds(r * slots + s, devices, stride=span), :] = value[
                    top : top + devices, left : left + 128
                ]


def over_groups(groups, body):
    sections = 4
    each = groups // sections
    for q in range(sections):
        first = q * (MODES // sections)
        lax.fori_loop(q * each, (q + 1) * each, functools.partial(body, first), 0)


def widen(filter_ref, first, copies):
    gain = filter_ref[first:, :].astype(F32)
    return jnp.concatenate([gain] * copies, 1)


def forward_kernel(per_group, src, anal, tsynth, filt, weight, out, scratch, back):
    devices, span, _ = src.shape
    groups, _, width = anal.shape
    height = width // per_group
    unpack(src, scratch)

    def body(first, g, carry):
        operand = gather_group(scratch, g, devices, span, per_group, height)
        spectrum = jnp.dot(anal[g, first:, :], operand, preferred_element_type=F32).astype(BF16)
        scaled = (spectrum.astype(F32) * widen(filt, first, 2 * per_group)).astype(BF16)
        mixed = [
            jnp.dot(
                scaled[:, j * 256 : (j + 1) * 256], weight[...], preferred_element_type=F32
            ).astype(BF16)
            for j in range(per_group)
        ]
        mixed = mixed[0] if per_group == 1 else jnp.concatenate(mixed, 1)
        value = jnp.dot(tsynth[g, :, first:], mixed, preferred_element_type=F32)
        scatter_group(value, back, g, devices, span, per_group, height)
        return carry

    over_groups(groups, body)
    pack(back, out)


def backward_kernel(
    per_group, src, gsrc, anal, synth, tanal, filt, weight, out, wgrad, fgrad, scratch, gscratch
):
    devices, span, _ = src.shape
    groups, _, width = anal.shape
    height = width // per_group
    unpack(src, scratch)
    unpack(gsrc, gscratch)
    wgrad[...] = jnp.zeros_like(wgrad)
    fgrad[...] = jnp.zeros_like(fgrad)

    def body(first, g, carry):
        operand = gather_group(scratch, g, devices, span, per_group, height)
        goperand = gather_group(gscratch, g, devices, span, per_group, height)
        gain = widen(filt, first, 2)
        outs = []
        spectrum = jnp.dot(anal[g, first:, :], operand, preferred_element_type=F32).astype(BF16)
        gmixed = jnp.dot(synth[g, first:, :], goperand, preferred_element_type=F32).astype(BF16)
        for j in range(per_group):
            lanes = slice(j * 256, (j + 1) * 256)
            spec = spectrum[:, lanes].astype(F32)
            scaled = (spec * gain).astype(BF16)
            gmix = gmixed[:, lanes]
            wgrad[...] += lax.dot_general(
                scaled, gmix, (((0,), (0,)), ((), ())), preferred_element_type=F32
            )
            gscaled = lax.dot_general(
                gmix, weight[...], (((1,), (1,)), ((), ())), preferred_element_type=F32
            )
            term = gscaled * spec
            fgrad[first:, :] += term[:, :128] + term[:, 128:]
            outs.append((gscaled * gain).astype(BF16))
        gspectrum = outs[0] if per_group == 1 else jnp.concatenate(outs, 1)
        value = jnp.dot(tanal[g, :, first:], gspectrum, preferred_element_type=F32)
        scatter_group(value, scratch, g, devices, span, per_group, height)
        return carry

    over_groups(groups, body)
    pack(scratch, out)


def gelu_slope(field):
    return 0.5 * (1.0 + lax.erf(field * (1.0 / math.sqrt(2.0)))) + field * jnp.exp(
        -0.5 * field * field
    ) * (1.0 / math.sqrt(2.0 * math.pi))


LON_CHUNK = 288


def merged(src):
    devices, span, width = src.shape
    return src[...].astype(F32).reshape(devices * span, width)


def slope_kernel(src, alpha, table, ttable, upstream, out, slope):
    lat_local, lon_count, channels = upstream.shape
    devices, span, _ = out.shape
    operand = (merged(src) * alpha[:, 0:1]).astype(BF16)

    def grid_rows(q, carry):
        rows = pl.ds(pl.multiple_of(q * LON_CHUNK, LON_CHUNK), LON_CHUNK)
        field = jnp.dot(ttable[rows, :], operand, preferred_element_type=F32)
        up = jnp.concatenate([upstream[a, rows, :] for a in range(lat_local)], 1)
        slope[rows, :] = (up.astype(F32) * gelu_slope(field)).astype(BF16)
        return carry

    lax.fori_loop(0, lon_count // LON_CHUNK, grid_rows, 0)
    chunk = 256

    def product(q, carry):
        rows = pl.ds(pl.multiple_of(q * chunk, chunk), chunk)
        value = jnp.dot(table[rows, :], slope[...], preferred_element_type=F32)
        value = (value * alpha[rows, 0:1]).astype(BF16)
        out[pl.ds(q * (chunk // span), chunk // span)] = value.reshape(
            chunk // span, span, value.shape[1]
        )
        return carry

    lax.fori_loop(0, 2 * MODES // chunk, product, 0)


def final_kernel(src, ttable, upstream, out):
    lat_local, lon_count, channels = upstream.shape
    operand = merged(src).astype(BF16)

    def grid_rows(q, carry):
        rows = pl.ds(pl.multiple_of(q * LON_CHUNK, LON_CHUNK), LON_CHUNK)
        value = jnp.dot(ttable[rows, :], operand, preferred_element_type=F32)
        for a in range(lat_local):
            part = value[:, a * channels : (a + 1) * channels]
            out[a, rows, :] = (part + upstream[a, rows, :].astype(F32)).astype(BF16)
        return carry

    lax.fori_loop(0, lon_count // LON_CHUNK, grid_rows, 0)


def mixing_matrix(mix_weight):
    upper = jnp.concatenate([mix_weight[0], mix_weight[1]], 1)
    lower = jnp.concatenate([-mix_weight[1], mix_weight[0]], 1)
    return jnp.concatenate([upper, lower], 0)


def fold_weight(block_grad):
    half = block_grad.shape[0] // 2
    real_part = block_grad[:half, :half] + block_grad[half:, half:]
    imag_part = block_grad[:half, half:] - block_grad[half:, :half]
    return jnp.concatenate([real_part, imag_part], 0)


def exchange(value):
    return lax.all_to_all(value, "space", split_axis=0, concat_axis=0, tiled=True)


def shape(dims, kind=BF16):
    return jax.ShapeDtypeStruct(dims, kind)


def body(grid_in, upstream, mix_weight, degree_filter):
    devices = lax.axis_size("space")
    me = lax.axis_index("space")
    lat_local, lon_count, channels = grid_in.shape
    lat_count = lat_local * devices
    slots = MODES // devices
    span = 2 * slots
    height = 64 if lat_count <= 64 else -(-lat_count // 128) * 128
    per_group = 128 // height if height < 128 else 1
    width = height * per_group
    groups = slots // per_group
    packet = shape((devices, span, lat_local * channels))

    table, ttable, fourier = pl.pallas_call(
        fourier_kernel,
        out_shape=(shape((2 * MODES, lon_count)), shape((lon_count, 2 * MODES)), packet),
        compiler_params=params(),
        name="fourier_stage",
    )(*base_tables(devices, lon_count), grid_in)
    spectral_in = exchange(fourier)

    lane = jnp.arange(width, dtype=jnp.int32)
    within = lane % height
    valid = within < lat_count
    latitude = jnp.where(valid, within % devices * lat_local + within // devices, 0)
    angles = latitude_angles(latitude, lat_count)
    group = jnp.minimum(jnp.arange(-(-groups // 8) * 8, dtype=jnp.int32), groups - 1)[:, None]
    orders = ((group * per_group + lane[None, :] // height) * devices + me).astype(F32)
    cosine = jnp.broadcast_to(jnp.cos(angles)[None, :], orders.shape)
    start = 0.5 * (jnp.log(2.0 * orders + 1.0) - math.log(2.0))
    start = start + 0.5 * (
        lax.lgamma(2.0 * orders + 1.0) - 2.0 * lax.lgamma(orders + 1.0) - orders * math.log(4.0)
    )
    start = start + orders * jnp.log(jnp.sin(angles))[None, :]
    weights = jnp.where(valid, math.pi / lat_count * jnp.sin(angles), 0.0)
    tall = shape((groups, MODES, width))
    flat = shape((groups, width, MODES))
    synth, anal, tsynth, tanal = pl.pallas_call(
        legendre_kernel,
        out_shape=(tall, tall, flat, flat),
        scratch_shapes=[pltpu.VMEM((width // 128, MODES * orders.shape[0], 128), F32)],
        compiler_params=params(),
        name="legendre_stage",
    )(
        orders,
        cosine,
        start,
        jnp.broadcast_to(weights[None, :], (8, width)),
        jnp.broadcast_to(weights[:, None], (width, 128)),
    )

    wide_weight = mixing_matrix(mix_weight)
    slab = pltpu.VMEM((lat_local, devices * span, 128), F32)
    grid_modes = pl.pallas_call(
        functools.partial(forward_kernel, per_group),
        out_shape=packet,
        scratch_shapes=[slab, slab],
        compiler_params=params(),
        name="forward_stage",
    )(spectral_in, anal, tsynth, degree_filter, wide_weight)
    returned = exchange(grid_modes)

    order, _ = row_phase(jnp.arange(2 * MODES, dtype=jnp.int32), devices, lon_count)
    alpha = jnp.broadcast_to(jnp.where(order == 0, 1.0, 2.0).astype(F32)[:, None], (2 * MODES, 128))
    gfourier = pl.pallas_call(
        slope_kernel,
        out_shape=packet,
        scratch_shapes=[pltpu.VMEM((lon_count, lat_local * channels), BF16)],
        compiler_params=params(),
        name="slope_stage",
    )(returned, alpha, table, ttable, upstream)
    gradient_in = exchange(gfourier)

    gfield_modes, weight_total, filter_total = pl.pallas_call(
        functools.partial(backward_kernel, per_group),
        out_shape=(packet, shape((2 * channels, 2 * channels), F32), shape((MODES, channels), F32)),
        scratch_shapes=[slab, slab],
        compiler_params=params(),
        name="backward_stage",
    )(spectral_in, gradient_in, anal, synth, tanal, degree_filter, wide_weight)
    gfield = exchange(gfield_modes)
    totals = jnp.concatenate(
        [fold_weight(weight_total) * (1.0 / MODES), filter_total * 0.125], 0
    ).reshape(devices, -1, channels)
    share = jnp.sum(exchange(totals), 0)
    summed = exchange(jnp.broadcast_to(share[None], (devices,) + share.shape))
    summed = summed.reshape(2 * channels + MODES, channels)

    grad_in = pl.pallas_call(
        final_kernel,
        out_shape=shape(grid_in.shape),
        compiler_params=params(),
        name="final_stage",
    )(gfield, ttable, upstream)
    return (
        grad_in,
        summed[: 2 * channels].reshape(2, channels, channels),
        summed[2 * channels :],
    )


def solution(mesh):
    return jax.shard_map(
        body,
        mesh=mesh,
        in_specs=(P(("groups", "space"), None, None), P(("groups", "space"), None, None), P(), P()),
        out_specs=(P(("groups", "space"), None, None), P("groups", None, None), P("groups", None)),
        check_vma=False,
    )
```

time: 472 us -> 198 us (0.42); the launches traced: 464 us -> 197 us
  local copies, waits for them, and re-layouts: 142 us -> 6.52 us
  other arithmetic: 87.9 us -> 10.7 us
  Pallas kernels: 0 us -> 66.4 us
  waiting for transfers between devices: 105 us -> 39.5 us
  matrix products: 57.6 us -> 0 us
  blocking collectives: 0 us -> 56.9 us
  loops' own time: 29.5 us -> 0 us
  between operations: 15.2 us -> 0.8 us
  starting transfers between devices: 27 us -> 16.4 us
    psum x1 -> x0, waiting for transfers between devices: 92.3 us -> none  [body(): lax.psum((weight_total * (1.0 / MODES), filter_total * 0.125), 'space')]
    pallas_call x0 -> x6, Pallas kernels: none -> 66.4 us  [the longest x1 17.5 us: body(): pl.pallas_call(functools.partial(backward_kernel, per_group), out_shape=(...]
    dot_general x31 -> x0, matrix products: 57.6 us -> none  [the longest x4 10.7 us: body(): jnp.dot(scaled_rows, wide_weight, preferred_element_type=jnp.float32)]
    all_to_all x0 -> x3, blocking collectives: none -> 56.9 us  [exchange(): lax.all_to_all(value, 'space', split_axis=0, concat_axis=0, tiled=True)]
    convert_element_type x15 -> x0, local copies, waits for them, and re-layouts: 47.3 us -> none  [the longest x8 24.9 us: body(): spectrum.astype(jnp.float32) * filter_gain[first_degree:][None, :, None, :]]
    while x496 -> x0, other arithmetic: 46.5 us -> none
    another operation x1 -> x0, loops' own time: 29.5 us -> none  [legendre_rows(): final_carry, stacked = lax.scan(degree_block, start_carry, block_ids)]
    all_to_all x4 -> x3, waiting for transfers between devices: 12.8 us -> 39.5 us  [exchange(): lax.all_to_all(value, 'space', split_axis=0, concat_axis=0, tiled=True)]
  transfers between devices with their start and end apart: 5 -> 3, of which waited for: 3 -> 3; matrix products, arithmetic and copies ran while one was open for 33% -> 3% of each run, Pallas kernels for 0% -> 5%
where the time goes in v1:
time: 198 us; the launch traced here: 197 us
  Pallas kernels  66.4 us (34%)
  blocking collectives  56.9 us (29%)
  waiting for transfers between devices  39.5 us (20%)
  starting transfers between devices  16.4 us (8%)
  other arithmetic  10.7 us (5%)
  local copies, waits for them, and re-layouts  6.52 us (3%)
    all_to_all x3, blocking collectives, exchange(): lax.all_to_all(value, 'space', split_axis=0, concat_axis=0, tiled=True)  56.9 us
    all_to_all x3, waiting for transfers between devices, exchange(): lax.all_to_all(value, 'space', split_axis=0, concat_axis=0, tiled=True)  39.5 us
    pallas_call x1, Pallas kernels, body(): pl.pallas_call(functools.partial(backward_kernel, per_group), out_shape=(...  17.5 us
    all_to_all x3, starting transfers between devices, exchange(): lax.all_to_all(value, 'space', split_axis=0, concat_axis=0, tiled=True)  16.4 us
    pallas_call x1, Pallas kernels, body(): pl.pallas_call(functools.partial(forward_kernel, per_group), out_shape=pa...  13.8 us
    pallas_call x1, Pallas kernels, body(): pl.pallas_call(legendre_kernel, out_shape=(tall, tall, flat, flat), scrat...  10.8 us
    pallas_call x1, Pallas kernels, body(): pl.pallas_call(slope_kernel, out_shape=packet, scratch_shapes=[pltpu.VMEM...  9.92 us
    pallas_call x1, Pallas kernels, body(): pl.pallas_call(fourier_kernel, out_shape=(shape((2 * MODES, lon_count)),...  8.54 us
  transfers between devices with their start and end apart: 3, of which 3 were waited for; matrix products, arithmetic and copies ran while one was open for 3% of the time, Pallas kernels for 5%

profile of v1, /device:TPU:0, one launch (start us, length us, event | category | flops | bytes accessed | tf_op | source)
XLA Modules:
  0.0 197.3 jit_solution(3567211614129143989)
XLA Ops:
  0.7 0.1 slice.56
  0.8 0.1 slice.57
  0.9 0.6 fusion.26
  1.5 0.1 slice.60
  1.7 0.9 fusion.9
  2.6 0.9 fusion.13
  3.5 0.8 maximum_multiply_fusion.fine
  4.3 0.7 maximum_multiply_fusion.1.tfine
  5.0 0.9 fusion.17
  5.9 0.8 pad_maximum_fusion.coarse
  6.7 0.8 pad_maximum_fusion.1.tcoarse
  7.4 0.0 copy-start.3
  7.4 8.5 %fourier_stage.1 = (bf16[1024,1440]{1,0:T(8,128)(2,1)}, bf16[1440,1024]{1,0:T(8,128)(2,1)}, bf16[16,64,384]{2,1,0:T(8,128)(2,1)}) custom-call(f32[2,32,1440]{2,1,0:T(8,128)} %pad_maximum_fusion.coarse, f32[2,32,1440]{2,1,0:T(8,128)} %maximum_multiply_fusion.fine, f32[2,45,1024]{2,1,0:T(8,128)} %pad_maximum_fusion.1.tcoarse, ...), custom_call_target="tpu_custom_call" | custom-call | tf_op jit(solution)/shard_map/fourier_stage/pallas_call | solution.py:352
  16.0 7.4 %all-to-all-start = ((bf16[16,64,384]{2,1,0:T(8,128)(2,1)}), bf16[16,64,384]{2,1,0:T(8,128)(2,1)S(1)}, u32[]{:S(2)}, u32[]{:S(2)}) async-start(bf16[16,64,384]{2,1,0:T(8,128)(2,1)} %get-tuple-element.13), calls=%async_computation | async-start | bytes 1572864 | tf_op jit(solution)/shard_map/all_to_all | solution.py:332
  23.4 0.1 fusion.55
  23.5 0.1 compare_select_fusion.6
  23.5 0.1 fusion.54
  23.6 0.7 add_convert_fusion.order_ref
  24.3 0.8 multiply_add_fusion.start_ref
  25.1 0.7 broadcast_in_dim.25.wcol_ref
  25.8 0.6 broadcast_in_dim.24.weight_ref
  26.4 0.6 broadcast_in_dim.22.cos_ref
  27.0 10.8 %legendre_stage.1 = (bf16[16,512,128]{2,1,0:T(8,128)(2,1)}, bf16[16,512,128]{2,1,0:T(8,128)(2,1)}, bf16[16,128,512]{2,1,0:T(8,128)(2,1)}, bf16[16,128,512]{2,1,0:T(8,128)(2,1)}) custom-call(f32[16,128]{1,0:T(8,128)} %add_convert_fusion.order_ref, f32[16,128]{1,0:T(8,128)} %broadcast_in_dim.22.cos_ref, f32[16,128]{1,0:T(8,128)} %multiply_add_fusion.start_ref, ...), custom_call_target="tpu_custom_call" | custom-call | tf_op jit(solution)/shard_map/legendre_stage/pallas_call | solution.py:376
  37.8 0.0 copy-done.3
  37.8 0.7 maximum_maximum_fusion.weight
  38.5 3.6 %all-to-all-done.src = bf16[16,64,384]{2,1,0:T(8,128)(2,1)S(1)} async-done(((bf16[16,64,384]{2,1,0:T(8,128)(2,1)}), bf16[16,64,384]{2,1,0:T(8,128)(2,1)S(1)}, u32[]{:S(2)}, u32[]{:S(2)}) %all-to-all-start) | async-done | bytes 786464 | tf_op jit(solution)/shard_map/all_to_all | solution.py:332
  42.1 0.0 copy-start
  42.1 0.9 copy-done
  43.0 13.8 %forward_stage.1 = bf16[16,64,384]{2,1,0:T(8,128)(2,1)} custom-call(bf16[16,64,384]{2,1,0:T(8,128)(2,1)} %copy-done, bf16[16,512,128]{2,1,0:T(8,128)(2,1)} %get-tuple-element.14.anal, bf16[16,128,512]{2,1,0:T(8,128)(2,1)} %get-tuple-element.15.tsynth, bf16[512,128]{1,0:T(8,128)(2,1)} %filt.3, bf16[256,256]{1,0:T(8,128)(2,1)} %maximum_maximum_fusion.weight), custom_call_target="tpu_custom_call" | custom-call | tf_op jit(solution)/shard_map/forward_stage/pallas_call | solution.py:392
  56.8 5.4 %all-to-all-start.1 = ((bf16[16,64,384]{2,1,0:T(8,128)(2,1)}), bf16[16,64,384]{2,1,0:T(8,128)(2,1)S(1)}, u32[]{:S(2)}, u32[]{:S(2)}) async-start(bf16[16,64,384]{2,1,0:T(8,128)(2,1)} %forward_stage.1), calls=%async_computation.1 | async-start | bytes 1572864 | tf_op jit(solution)/shard_map/all_to_all | solution.py:332
  62.2 18.7 %all-to-all-done.1.src = bf16[16,64,384]{2,1,0:T(8,128)(2,1)S(1)} async-done(((bf16[16,64,384]{2,1,0:T(8,128)(2,1)}), bf16[16,64,384]{2,1,0:T(8,128)(2,1)S(1)}, u32[]{:S(2)}, u32[]{:S(2)}) %all-to-all-start.1) | async-done | bytes 786464 | tf_op jit(solution)/shard_map/all_to_all | solution.py:332
  80.9 0.0 copy-start.2
  80.9 1.1 broadcast_in_dim.28.alpha
  81.9 0.0 copy-done.2
  81.9 9.9 %slope_stage.1 = bf16[16,64,384]{2,1,0:T(8,128)(2,1)} custom-call(bf16[16,64,384]{2,1,0:T(8,128)(2,1)} %copy-done.2, f32[1024,128]{1,0:T(8,128)} %broadcast_in_dim.28.alpha, bf16[1024,1440]{1,0:T(8,128)(2,1)} %get-tuple-element.16.table, bf16[1440,1024]{1,0:T(8,128)(2,1)} %get-tuple-element.17.ttable, bf16[3,1440,128]{2,1,0:T(8,128)(2,1)} %upstream.3), custom_call_target="tpu_custom_call" | custom-call | tf_op jit(solution)/shard_map/slope_stage/pallas_call | solution.py:403
  91.8 25.6 %all_to_all.30.gsrc = bf16[16,64,384]{2,1,0:T(8,128)(2,1)} all-to-all(bf16[16,64,384]{2,1,0:T(8,128)(2,1)} %slope_stage.1), channel_id=1, replica_groups=mesh['groups'=2,'space'=16] {'space'}, dimensions={0} | all-to-all | bytes 1572864 | tf_op jit(solution)/shard_map/all_to_all | solution.py:332
  117.5 17.5 %backward_stage.1 = (bf16[16,64,384]{2,1,0:T(8,128)(2,1)}, f32[256,256]{1,0:T(8,128)}, f32[512,128]{1,0:T(8,128)}) custom-call(bf16[16,64,384]{2,1,0:T(8,128)(2,1)} %copy-done, bf16[16,64,384]{2,1,0:T(8,128)(2,1)} %all_to_all.30.gsrc, bf16[16,512,128]{2,1,0:T(8,128)(2,1)} %get-tuple-element.14.anal, bf16[16,512,128]{2,1,0:T(8,128)(2,1)} %get-tuple-element.18.synth, ...), custom_call_target="tpu_custom_call" | custom-call | tf_op jit(solution)/shard_map/backward_stage/pallas_call | solution.py:412
  135.0 0.9 slice_add_fusion
  135.9 1.0 broadcast_multiply_fusion
  137.0 15.9 %all_to_all.31 = f32[16,48,128]{2,1,0:T(8,128)S(1)} all-to-all(f32[16,48,128]{2,1,0:T(8,128)S(1)} %bitcast.11), channel_id=1, replica_groups=mesh['groups'=2,'space'=16] {'space'}, dimensions={0} | all-to-all | bytes 786432 | tf_op jit(solution)/shard_map/all_to_all | solution.py:332
  152.9 15.4 %all_to_all.32 = f32[16,48,128]{2,1,0:T(8,128)S(1)} all-to-all(f32[16,48,128]{2,1,0:T(8,128)S(1)} %broadcast_in_dim.29), channel_id=1, replica_groups=mesh['groups'=2,'space'=16] {'space'}, dimensions={0} | all-to-all | bytes 786432 | tf_op jit(solution)/shard_map/all_to_all | solution.py:332
  168.3 3.6 %all-to-all-start.3 = ((bf16[16,64,384]{2,1,0:T(8,128)(2,1)}), bf16[16,64,384]{2,1,0:T(8,128)(2,1)S(1)}, u32[]{:S(2)}, u32[]{:S(2)}) async-start(bf16[16,64,384]{2,1,0:T(8,128)(2,1)} %get-tuple-element.20), calls=%async_computation.3 | async-start | bytes 1572864 | tf_op jit(solution)/shard_map/all_to_all | solution.py:332
  171.9 0.7 slice.71
  172.7 0.7 slice.70
  173.3 17.3 %all-to-all-done.3.src = bf16[16,64,384]{2,1,0:T(8,128)(2,1)S(1)} async-done(((bf16[16,64,384]{2,1,0:T(8,128)(2,1)}), bf16[16,64,384]{2,1,0:T(8,128)(2,1)S(1)}, u32[]{:S(2)}, u32[]{:S(2)}) %all-to-all-start.3) | async-done | bytes 786464 | tf_op jit(solution)/shard_map/all_to_all | solution.py:332
  190.6 0.0 copy-start.1
  190.6 0.9 copy-done.1
  191.5 5.8 %final_stage.1 = bf16[3,1440,128]{2,1,0:T(8,128)(2,1)} custom-call(bf16[16,64,384]{2,1,0:T(8,128)(2,1)} %copy-done.1, bf16[1440,1024]{1,0:T(8,128)(2,1)} %get-tuple-element.17.ttable, bf16[3,1440,128]{2,1,0:T(8,128)(2,1)} %upstream.3), custom_call_target="tpu_custom_call" | custom-call | tf_op jit(solution)/shard_map/final_stage/pallas_call | solution.py:427
  (14 shorter events, 0.1 us)
Async XLA Ops:
  7.4 30.3 %copy-start.3 = (bf16[2,128,128]{2,1,0:T(8,128)(2,1)S(1)}, bf16[2,128,128]{2,1,0:T(8,128)(2,1)}, u32[]{:S(2)}) copy-start(bf16[2,128,128]{2,1,0:T(8,128)(2,1)} %param.6) | copy-start | bytes 196612
  16.0 26.1 %all-to-all-start = ((bf16[16,64,384]{2,1,0:T(8,128)(2,1)}), bf16[16,64,384]{2,1,0:T(8,128)(2,1)S(1)}, u32[]{:S(2)}, u32[]{:S(2)}) async-start(bf16[16,64,384]{2,1,0:T(8,128)(2,1)} %get-tuple-element.13), calls=%async_computation | async-start | bytes 1572864 | tf_op jit(solution)/shard_map/all_to_all | solution.py:332
  42.1 0.9 copy-start
  56.8 24.1 %all-to-all-start.1 = ((bf16[16,64,384]{2,1,0:T(8,128)(2,1)}), bf16[16,64,384]{2,1,0:T(8,128)(2,1)S(1)}, u32[]{:S(2)}, u32[]{:S(2)}) async-start(bf16[16,64,384]{2,1,0:T(8,128)(2,1)} %forward_stage.1), calls=%async_computation.1 | async-start | bytes 1572864 | tf_op jit(solution)/shard_map/all_to_all | solution.py:332
  80.9 1.1 copy-start.2
  168.3 22.3 %all-to-all-start.3 = ((bf16[16,64,384]{2,1,0:T(8,128)(2,1)}), bf16[16,64,384]{2,1,0:T(8,128)(2,1)S(1)}, u32[]{:S(2)}, u32[]{:S(2)}) async-start(bf16[16,64,384]{2,1,0:T(8,128)(2,1)} %get-tuple-element.20), calls=%async_computation.3 | async-start | bytes 1572864 | tf_op jit(solution)/shard_map/all_to_all | solution.py:332
  190.6 0.9 copy-start.1

commit v2 on v1

--- a/solution.py
+++ b/solution.py
@@ -22,12 +22,131 @@
     return math.pi * (index.astype(F32) + 0.5) / lat_count
 
 
+def greet(devices):
+    me = lax.axis_index("space")
+    barrier = pltpu.get_barrier_semaphore()
+
+    def hello(step, carry):
+        peer = (me + step) % devices
+        pl.semaphore_signal(
+            barrier, inc=1, device_id={"space": peer}, device_id_type=pl.DeviceIdType.MESH
+        )
+        return carry
+
+    lax.fori_loop(1, devices, hello, 0)
+
+
+def await_greetings(devices):
+    pl.semaphore_wait(pltpu.get_barrier_semaphore(), devices - 1)
+
+
+def remote(src, dst, send_sem, recv_sem, peer):
+    return pltpu.make_async_remote_copy(
+        src_ref=src,
+        dst_ref=dst,
+        send_sem=send_sem,
+        recv_sem=recv_sem,
+        device_id={"space": peer},
+        device_id_type=pl.DeviceIdType.MESH,
+    )
+
+
+class Exchange:
+    def __init__(self, source, target, send_sem, recv_sem):
+        self.source, self.target = source, target
+        self.send_sem, self.recv_sem = send_sem, recv_sem
+        self.devices = source.shape[1]
+        self.me = lax.axis_index("space")
+
+    def copy(self, section, step):
+        peer = (self.me + step) % self.devices
+        return remote(
+            self.source.at[section, peer],
+            self.target.at[section, self.me],
+            self.send_sem.at[section, step],
+            self.recv_sem.at[section, step],
+            peer,
+        )
+
+    def send(self, section):
+        half = self.devices // 2
+
+        def one(index, carry):
+            sign = 1 - 2 * (index % 2)
+            step = (half + sign * ((index + 1) // 2) + self.devices) % self.devices
+            self.copy(section, step).start()
+            return carry
+
+        lax.fori_loop(0, self.devices - 1, one, 0)
+        self.target[section, self.me] = self.source[section, self.me]
+
+    def finish(self):
+        for section in range(self.source.shape[0]):
+
+            def one(step, carry, section=section):
+                copy = self.copy(section, step)
+                copy.wait_recv()
+                copy.wait_send()
+                return carry
+
+            lax.fori_loop(1, self.devices, one, 0)
+
+
+def reduce_all(red, inbox, total, send_sem, recv_sem):
+    devices = red.shape[0]
+    me = lax.axis_index("space")
+    base = me * 0
+    steps = []
+    stride = 1
+    while stride < devices:
+        half = devices // (2 * stride)
+        bit = me // stride % 2
+        partner = me + (1 - 2 * bit) * stride
+        steps.append((half, bit, partner))
+        stride *= 2
+    trail = []
+    for t, (half, bit, partner) in enumerate(steps):
+        keep = base + bit * half
+        give = base + (1 - bit) * half
+        copy = remote(
+            red.at[pl.ds(give, half)],
+            inbox.at[pl.ds(half, half)],
+            send_sem.at[t],
+            recv_sem.at[t],
+            partner,
+        )
+        copy.start()
+        copy.wait()
+        red[pl.ds(keep, half)] += inbox[half : 2 * half]
+        base = keep
+        trail.append(base)
+    total[pl.ds(base, 1)] = red[pl.ds(base, 1)]
+    count = len(steps)
+    for t in reversed(range(count)):
+        half, bit, partner = steps[t]
+        block = pl.ds(trail[t], half)
+        copy = remote(
+            total.at[block],
+            total.at[block],
+            send_sem.at[count + t],
+            recv_sem.at[count + t],
+            partner,
+        )
+        copy.start()
+        copy.wait()
+
+
+def sections_of(devices):
+    return max(1, min(4, MODES // devices // 8))
+
+
 def row_phase(rows, devices, lon_count):
-    slots = MODES // devices
-    device = rows // (2 * slots)
-    part = rows // slots % 2
-    order = rows % slots * devices + device
-    return order, part * (lon_count // 4)
+    span = 2 * MODES // devices // sections_of(devices)
+    section = rows // (span * devices)
+    device = rows // span % devices
+    part = rows // (span // 2) % 2
+    slot = section * (span // 2) + rows % (span // 2)
+    return slot * devices + device, part * (lon_count // 4)
 
 
 def trig(phases, lon_count):
@@ -52,34 +171,56 @@
     )
 
 
-def fourier_kernel(coarse, fine, tcoarse, tfine, grid, table, ttable, out):
-    lat_local = grid.shape[0]
-    devices, span = out.shape[0], out.shape[1]
-
-    def fill(dst, big, small):
-        def step(h, carry):
-            value = big[0, pl.ds(h, 1), :] * small[0] - big[1, pl.ds(h, 1), :] * small[1]
-            dst[pl.ds(pl.multiple_of(h * ROWS, ROWS), ROWS), :] = value.astype(BF16)
-            return carry
-
-        lax.fori_loop(0, big.shape[1], step, 0)
-
+def fill(dst, big, small):
+    def step(h, carry):
+        value = big[0, pl.ds(h, 1), :] * small[0] - big[1, pl.ds(h, 1), :] * small[1]
+        dst[pl.ds(pl.multiple_of(h * ROWS, ROWS), ROWS), :] = value.astype(BF16)
+        return carry
+
+    lax.fori_loop(0, big.shape[1], step, 0)
+
+
+def section_product(table, wide, out, section, scale=None):
+    _, devices, span, width = out.shape
+    chunk = 256
+    each = chunk // span
+
+    def product(q, carry):
+        rows = pl.ds(pl.multiple_of(section * devices * span + q * chunk, chunk), chunk)
+        value = jnp.dot(table[rows, :], wide, preferred_element_type=F32)
+        if scale is not None:
+            value = value * scale[rows, 0:1]
+        out[section, pl.ds(q * each, each)] = value.astype(BF16).reshape(each, span, width)
+        return carry
+
+    lax.fori_loop(0, devices * span // chunk, product, 0)
+
+
+def fourier_kernel(
+    coarse, fine, tcoarse, tfine, grid, order_ref, cos_ref, start_ref, weight_ref, wcol_ref,
+    table, ttable, received, synth, anal, tsynth, tanal,
+    out, hold, send_sem, recv_sem,
+):
+    sections, devices = out.shape[:2]
+    greet(devices)
     fill(table, coarse, fine)
+    wide = jnp.concatenate([grid[a] for a in range(grid.shape[0])], 1)
+    exchange = Exchange(out, received, send_sem, recv_sem)
+    for section in range(sections):
+        section_product(table, wide, out, section)
+        if section == 0:
+            await_greetings(devices)
+        exchange.send(section)
+    legendre_tables(
+        order_ref, cos_ref, start_ref, weight_ref, wcol_ref, synth, anal, tsynth, tanal, hold
+    )
     fill(ttable, tcoarse, tfine)
-    wide = jnp.concatenate([grid[a] for a in range(lat_local)], 1)
-    chunk = 256
-
-    def product(q, carry):
-        rows = pl.ds(pl.multiple_of(q * chunk, chunk), chunk)
-        value = jnp.dot(table[rows, :], wide, preferred_element_type=F32)
-        value = value.astype(BF16).reshape(chunk // span, span, value.shape[1])
-        out[pl.ds(q * (chunk // span), chunk // span)] = value
-        return carry
-
-    lax.fori_loop(0, 2 * MODES // chunk, product, 0)
-
-
-def legendre_kernel(order_ref, cos_ref, start_ref, weight_ref, wcol_ref, synth, anal, tsynth, tanal, hold):
+    exchange.finish()
+
+
+def legendre_tables(
+    order_ref, cos_ref, start_ref, weight_ref, wcol_ref, synth, anal, tsynth, tanal, hold
+):
     groups, width = order_ref.shape
     orders = order_ref[...]
     order_sq = orders * orders
@@ -131,31 +272,37 @@
 
 
 def unpack(src, scratch):
-    devices, span, _ = src.shape
+    sections, devices, span, _ = src.shape
+    for q in range(sections):
+        for a in range(scratch.shape[0]):
+            part = src[q, :, :, a * 128 : (a + 1) * 128].astype(F32)
+            scratch[a, q * devices * span : (q + 1) * devices * span] = part.reshape(
+                devices * span, 128
+            )
+
+
+def pack(scratch, dst, q):
+    _, devices, span, _ = dst.shape
     for a in range(scratch.shape[0]):
-        part = src[:, :, a * 128 : (a + 1) * 128].astype(F32)
-        scratch[a] = part.reshape(devices * span, 128)
-
-
-def pack(scratch, dst):
-    devices, span, _ = dst.shape
-    for a in range(scratch.shape[0]):
-        dst[:, :, a * 128 : (a + 1) * 128] = (
-            scratch[a].reshape(devices, span, 128).astype(BF16)
-        )
+        part = scratch[a, q * devices * span : (q + 1) * devices * span]
+        dst[q, :, :, a * 128 : (a + 1) * 128] = part.reshape(devices, span, 128).astype(BF16)
+
+
+def strided_rows(s, r, devices, span):
+    half = span // 2
+    start = s // half * (devices * span) + r * half + s % half
+    return pl.ds(start, devices, stride=span)
 
 
 def gather_group(scratch, g, devices, span, per_group, height):
     lat_local = scratch.shape[0]
-    slots = span // 2
     rows = []
     for j in range(per_group):
         s = g * per_group + j
         halves = []
         for r in range(2):
-            parts = [
-                scratch[a, pl.ds(r * slots + s, devices, stride=span), :] for a in range(lat_local)
-            ]
+            pick = strided_rows(s, r, devices, span)
+            parts = [scratch[a, pick, :] for a in range(lat_local)]
             if height > devices * lat_local:
                 parts.append(jnp.zeros((height - devices * lat_local, 128), F32))
             halves.append(jnp.concatenate(parts, 0))
@@ -168,24 +315,25 @@
 
 def scatter_group(value, scratch, g, devices, span, per_group, height):
     lat_local = scratch.shape[0]
-    slots = span // 2
     for j in range(per_group):
         s = g * per_group + j
         for r in range(2):
             for a in range(lat_local):
                 top = j * height + a * devices
                 left = j * 256 + r * 128
-                scratch[a, pl.ds(r * slots + s, devices, stride=span), :] = value[
+                scratch[a, strided_rows(s, r, devices, span), :] = value[
                     top : top + devices, left : left + 128
                 ]
 
 
-def over_groups(groups, body):
-    sections = 4
-    each = groups // sections
-    for q in range(sections):
-        first = q * (MODES // sections)
+def over_groups(groups, sections, body, after):
+    pieces = 4
+    each = groups // pieces
+    for q in range(pieces):
+        first = q * (MODES // pieces)
         lax.fori_loop(q * each, (q + 1) * each, functools.partial(body, first), 0)
+        if (q + 1) % (pieces // sections) == 0:
+            after(q // (pieces // sections))
 
 
 def widen(filter_ref, first, copies):
@@ -193,11 +341,15 @@
     return jnp.concatenate([gain] * copies, 1)
 
 
-def forward_kernel(per_group, src, anal, tsynth, filt, weight, out, scratch, back):
-    devices, span, _ = src.shape
+def forward_kernel(
+    per_group, src, anal, tsynth, filt, weight, received, out, scratch, back, send_sem, recv_sem
+):
+    sections, devices, span, _ = src.shape
     groups, _, width = anal.shape
     height = width // per_group
+    greet(devices)
     unpack(src, scratch)
+    exchange = Exchange(out, received, send_sem, recv_sem)
 
     def body(first, g, carry):
         operand = gather_group(scratch, g, devices, span, per_group, height)
@@ -214,20 +366,29 @@
         scatter_group(value, back, g, devices, span, per_group, height)
         return carry
 
-    over_groups(groups, body)
-    pack(back, out)
+    def after(q):
+        pack(back, out, q)
+        if q == 0:
+            await_greetings(devices)
+        exchange.send(q)
+
+    over_groups(groups, sections, body, after)
+    exchange.finish()
 
 
 def backward_kernel(
-    per_group, src, gsrc, anal, synth, tanal, filt, weight, out, wgrad, fgrad, scratch, gscratch
+    per_group, src, gsrc, anal, synth, tanal, filt, weight, received, total,
+    out, scratch, gscratch, wgrad, fgrad, red, inbox, send_sem, recv_sem, rsend_sem, rrecv_sem,
 ):
-    devices, span, _ = src.shape
+    sections, devices, span, _ = src.shape
     groups, _, width = anal.shape
     height = width // per_group
+    greet(devices)
     unpack(src, scratch)
     unpack(gsrc, gscratch)
     wgrad[...] = jnp.zeros_like(wgrad)
     fgrad[...] = jnp.zeros_like(fgrad)
+    exchange = Exchange(out, received, send_sem, recv_sem)
 
     def body(first, g, carry):
         operand = gather_group(scratch, g, devices, span, per_group, height)
@@ -255,8 +416,25 @@
         scatter_group(value, scratch, g, devices, span, per_group, height)
         return carry
 
-    over_groups(groups, body)
-    pack(scratch, out)
+    def after(q):
+        pack(scratch, out, q)
+        if q == 0:
+            await_greetings(devices)
+        exchange.send(q)
+
+    over_groups(groups, sections, body, after)
+    half = wgrad.shape[0] // 2
+    pieces = [
+        (wgrad[:half, :half] + wgrad[half:, half:]) * (1.0 / MODES),
+        (wgrad[:half, half:] - wgrad[half:, :half]) * (1.0 / MODES),
+        fgrad[...] * 0.125,
+    ]
+    spare = red.shape[0] * red.shape[1] - 2 * half - MODES
+    if spare:
+        pieces.append(jnp.zeros((spare, 128), F32))
+    red[...] = jnp.concatenate(pieces, 0).reshape(red.shape)
+    reduce_all(red, inbox, total, rsend_sem, rrecv_sem)
+    exchange.finish()
 
 
 def gelu_slope(field):
@@ -269,13 +447,14 @@
 
 
 def merged(src):
-    devices, span, width = src.shape
-    return src[...].astype(F32).reshape(devices * span, width)
-
-
-def slope_kernel(src, alpha, table, ttable, upstream, out, slope):
+    sections, devices, span, width = src.shape
+    return src[...].astype(F32).reshape(sections * devices * span, width)
+
+
+def slope_kernel(src, alpha, table, ttable, upstream, received, out, slope, send_sem, recv_sem):
     lat_local, lon_count, channels = upstream.shape
-    devices, span, _ = out.shape
+    sections, devices = out.shape[:2]
+    greet(devices)
     operand = (merged(src) * alpha[:, 0:1]).astype(BF16)
 
     def grid_rows(q, carry):
@@ -286,18 +465,12 @@
         return carry
 
     lax.fori_loop(0, lon_count // LON_CHUNK, grid_rows, 0)
-    chunk = 256
-
-    def product(q, carry):
-        rows = pl.ds(pl.multiple_of(q * chunk, chunk), chunk)
-        value = jnp.dot(table[rows, :], slope[...], preferred_element_type=F32)
-        value = (value * alpha[rows, 0:1]).astype(BF16)
-        out[pl.ds(q * (chunk // span), chunk // span)] = value.reshape(
-            chunk // span, span, value.shape[1]
-        )
-        return carry
-
-    lax.fori_loop(0, 2 * MODES // chunk, product, 0)
+    await_greetings(devices)
+    exchange = Exchange(out, received, send_sem, recv_sem)
+    for section in range(sections):
+        section_product(table, slope[...], out, section, alpha)
+        exchange.send(section)
+    exchange.finish()
 
 
 def final_kernel(src, ttable, upstream, out):
@@ -321,17 +494,6 @@
     return jnp.concatenate([upper, lower], 0)
 
 
-def fold_weight(block_grad):
-    half = block_grad.shape[0] // 2
-    real_part = block_grad[:half, :half] + block_grad[half:, half:]
-    imag_part = block_grad[:half, half:] - block_grad[half:, :half]
-    return jnp.concatenate([real_part, imag_part], 0)
-
-
-def exchange(value):
-    return lax.all_to_all(value, "space", split_axis=0, concat_axis=0, tiled=True)
-
-
 def shape(dims, kind=BF16):
     return jax.ShapeDtypeStruct(dims, kind)
 
@@ -342,20 +504,16 @@
     lat_local, lon_count, channels = grid_in.shape
     lat_count = lat_local * devices
     slots = MODES // devices
-    span = 2 * slots
+    sections = sections_of(devices)
+    span = 2 * slots // sections
     height = 64 if lat_count <= 64 else -(-lat_count // 128) * 128
     per_group = 128 // height if height < 128 else 1
     width = height * per_group
     groups = slots // per_group
-    packet = shape((devices, span, lat_local * channels))
-
-    table, ttable, fourier = pl.pallas_call(
-        fourier_kernel,
-        out_shape=(shape((2 * MODES, lon_count)), shape((lon_count, 2 * MODES)), packet),
-        compiler_params=params(),
-        name="fourier_stage",
-    )(*base_tables(devices, lon_count), grid_in)
-    spectral_in = exchange(fourier)
+    dims = (sections, devices, span, lat_local * channels)
+    packet = shape(dims)
+    outgoing = pltpu.VMEM(dims, BF16)
+    semaphores = pltpu.SemaphoreType.DMA((sections, devices))
 
     lane = jnp.arange(width, dtype=jnp.int32)
     within = lane % height
@@ -373,13 +531,28 @@
     weights = jnp.where(valid, math.pi / lat_count * jnp.sin(angles), 0.0)
     tall = shape((groups, MODES, width))
     flat = shape((groups, width, MODES))
-    synth, anal, tsynth, tanal = pl.pallas_call(
-        legendre_kernel,
-        out_shape=(tall, tall, flat, flat),
-        scratch_shapes=[pltpu.VMEM((width // 128, MODES * orders.shape[0], 128), F32)],
-        compiler_params=params(),
-        name="legendre_stage",
+    table, ttable, spectral_in, synth, anal, tsynth, tanal = pl.pallas_call(
+        fourier_kernel,
+        out_shape=(
+            shape((2 * MODES, lon_count)),
+            shape((lon_count, 2 * MODES)),
+            packet,
+            tall,
+            tall,
+            flat,
+            flat,
+        ),
+        scratch_shapes=[
+            outgoing,
+            pltpu.VMEM((width // 128, MODES * orders.shape[0], 128), F32),
+            semaphores,
+            semaphores,
+        ],
+        compiler_params=params(collective_id=0, has_side_effects=True),
+        name="fourier_stage",
     )(
+        *base_tables(devices, lon_count),
+        grid_in,
         orders,
         cosine,
         start,
@@ -388,41 +561,53 @@
     )
 
     wide_weight = mixing_matrix(mix_weight)
-    slab = pltpu.VMEM((lat_local, devices * span, 128), F32)
-    grid_modes = pl.pallas_call(
+    slab = pltpu.VMEM((lat_local, 2 * MODES, 128), F32)
+    returned = pl.pallas_call(
         functools.partial(forward_kernel, per_group),
         out_shape=packet,
-        scratch_shapes=[slab, slab],
-        compiler_params=params(),
+        scratch_shapes=[outgoing, slab, slab, semaphores, semaphores],
+        compiler_params=params(collective_id=1, has_side_effects=True),
         name="forward_stage",
     )(spectral_in, anal, tsynth, degree_filter, wide_weight)
-    returned = exchange(grid_modes)
 
     order, _ = row_phase(jnp.arange(2 * MODES, dtype=jnp.int32), devices, lon_count)
     alpha = jnp.broadcast_to(jnp.where(order == 0, 1.0, 2.0).astype(F32)[:, None], (2 * MODES, 128))
-    gfourier = pl.pallas_call(
+    gradient_in = pl.pallas_call(
         slope_kernel,
         out_shape=packet,
-        scratch_shapes=[pltpu.VMEM((lon_count, lat_local * channels), BF16)],
-        compiler_params=params(),
+        scratch_shapes=[
+            outgoing,
+            pltpu.VMEM((lon_count, lat_local * channels), BF16),
+            semaphores,
+            semaphores,
+        ],
+        compiler_params=params(collective_id=2, has_side_effects=True),
         name="slope_stage",
     )(returned, alpha, table, ttable, upstream)
-    gradient_in = exchange(gfourier)
-
-    gfield_modes, weight_total, filter_total = pl.pallas_call(
+
+    share = -(-(2 * channels + MODES) // (8 * devices)) * 8
+    blocks = (devices, share, channels)
+    hops = pltpu.SemaphoreType.DMA((2 * devices.bit_length(),))
+    gfield, summed = pl.pallas_call(
         functools.partial(backward_kernel, per_group),
-        out_shape=(packet, shape((2 * channels, 2 * channels), F32), shape((MODES, channels), F32)),
-        scratch_shapes=[slab, slab],
-        compiler_params=params(),
+        out_shape=(packet, shape(blocks, F32)),
+        scratch_shapes=[
+            outgoing,
+            slab,
+            slab,
+            pltpu.VMEM((2 * channels, 2 * channels), F32),
+            pltpu.VMEM((MODES, channels), F32),
+            pltpu.VMEM(blocks, F32),
+            pltpu.VMEM(blocks, F32),
+            semaphores,
+            semaphores,
+            hops,
+            hops,
+        ],
+        compiler_params=params(collective_id=3, has_side_effects=True),
         name="backward_stage",
     )(spectral_in, gradient_in, anal, synth, tanal, degree_filter, wide_weight)
-    gfield = exchange(gfield_modes)
-    totals = jnp.concatenate(
-        [fold_weight(weight_total) * (1.0 / MODES), filter_total * 0.125], 0
-    ).reshape(devices, -1, channels)
-    share = jnp.sum(exchange(totals), 0)
-    summed = exchange(jnp.broadcast_to(share[None], (devices,) + share.shape))
-    summed = summed.reshape(2 * channels + MODES, channels)
+    summed = summed.reshape(devices * share, channels)
 
     grad_in = pl.pallas_call(
         final_kernel,
@@ -433,7 +618,7 @@
     return (
         grad_in,
         summed[: 2 * channels].reshape(2, channels, channels),
-        summed[2 * channels :],
+        summed[2 * channels : 2 * channels + MODES],
     )
 
 

time: 198 us -> 150 us (0.76)
  Pallas kernels: 66.4 us -> 136 us
  blocking collectives: 56.9 us -> 0 us
  waiting for transfers between devices: 39.5 us -> 0 us
  starting transfers between devices: 16.4 us -> 0 us
    all_to_all x3 -> x0, blocking collectives: 56.9 us -> none  [exchange(): lax.all_to_all(value, 'space', split_axis=0, concat_axis=0, tiled=True)]
    all_to_all x3 -> x0, waiting for transfers between devices: 39.5 us -> none  [exchange(): lax.all_to_all(value, 'space', split_axis=0, concat_axis=0, tiled=True)]
    pallas_call x1, Pallas kernels: 17.5 us -> 43.3 us  [body(): pl.pallas_call(functools.partial(backward_kernel, per_group), out_shape=(...]
    pallas_call x1, Pallas kernels: 8.54 us -> 32.2 us  [body(): pl.pallas_call(fourier_kernel, out_shape=(shape((2 * MODES, lon_count)),...]
    all_to_all x3 -> x0, starting transfers between devices: 16.4 us -> none  [exchange(): lax.all_to_all(value, 'space', split_axis=0, concat_axis=0, tiled=True)]
    pallas_call x1, Pallas kernels: 13.8 us -> 26.1 us  [body(): pl.pallas_call(functools.partial(forward_kernel, per_group), out_shape=pa...]
    pallas_call x2 -> x1, Pallas kernels: 20.7 us -> 28.5 us  [body(): pl.pallas_call(slope_kernel, out_shape=packet, scratch_shapes=[outgoing,...]
  transfers between devices with their start and end apart: 3 -> 0, of which waited for: 3 -> 0; matrix products, arithmetic and copies ran while one was open for 3% -> 0% of each run, Pallas kernels for 5% -> 0%
where the time goes in v2:
time: 150 us
  Pallas kernels  136 us (91%)
  other arithmetic  8.75 us (6%)
  local copies, waits for them, and re-layouts  4.67 us (3%)
    pallas_call x1, Pallas kernels, body(): pl.pallas_call(functools.partial(backward_kernel, per_group), out_shape=(...  43.3 us
    pallas_call x1, Pallas kernels, body(): pl.pallas_call(fourier_kernel, out_shape=(shape((2 * MODES, lon_count)),...  32.2 us
    pallas_call x1, Pallas kernels, body(): pl.pallas_call(slope_kernel, out_shape=packet, scratch_shapes=[outgoing,...  28.5 us
    pallas_call x1, Pallas kernels, body(): pl.pallas_call(functools.partial(forward_kernel, per_group), out_shape=pa...  26.1 us
    pallas_call x1, Pallas kernels, body(): pl.pallas_call(final_kernel, out_shape=shape(grid_in.shape), compiler_par...  5.83 us
    cos x4, other arithmetic, trig(): return jnp.stack([jnp.cos(angles), jnp.sin(angles)], 0)  3.34 us

profile of v2, /device:TPU:0, one launch (start us, length us, event | category | flops | bytes accessed | tf_op | source)
XLA Modules:
  0.0 150.1 jit_solution(13694976807666951110)
XLA Ops:
  0.7 0.9 fusion.13
  1.6 0.8 maximum_multiply_fusion.fine
  2.4 0.6 fusion.26
  3.0 0.7 maximum_multiply_fusion.1.tfine
  3.7 0.1 slice.44
  3.9 0.1 slice.45
  4.0 0.9 fusion.17
  4.9 0.8 pad_maximum_fusion.coarse
  5.7 0.0 copy-start.1
  5.7 0.1 slice.48
  5.8 0.9 fusion.9
  6.7 0.8 pad_maximum_fusion.1.tcoarse
  7.5 0.1 fusion.60
  7.5 0.8 multiply_add_fusion.start_ref
  8.3 0.7 add_convert_fusion.order_ref
  9.0 0.1 compare_select_fusion.6
  9.1 0.7 broadcast_in_dim.23.wcol_ref
  9.8 0.6 broadcast_in_dim.22.weight_ref
  10.4 0.1 fusion.59
  10.4 0.6 broadcast_in_dim.20.cos_ref
  11.0 32.2 %fourier_stage.1 = (bf16[1024,1440]{1,0:T(8,128)(2,1)}, bf16[1440,1024]{1,0:T(8,128)(2,1)}, bf16[4,16,16,384]{3,2,1,0:T(8,128)(2,1)}, bf16[16,512,128]{2,1,0:T(8...) custom-call(f32[2,32,1440]{2,1,0:T(8,128)} %pad_maximum_fusion.coarse, ...), custom_call_target="tpu_custom_call" | custom-call | tf_op jit(solution)/shard_map/fourier_stage/pallas_call | solution.py:534
  43.2 0.0 copy-done.1
  43.2 0.7 maximum_maximum_fusion.weight
  43.9 26.1 %forward_stage.1.src = bf16[4,16,16,384]{3,2,1,0:T(8,128)(2,1)} custom-call(bf16[4,16,16,384]{3,2,1,0:T(8,128)(2,1)} %get-tuple-element.12.src, bf16[16,512,128]{2,1,0:T(8,128)(2,1)} %get-tuple-element.13.anal, bf16[16,128,512]{2,1,0:T(8,128)(2,1)} %get-tuple-element.14.tsynth, bf16[512,128]{1,0:T(8,128)(2,1)} %filt.3, ...), custom_call_target="tpu_custom_call" | custom-call | tf_op jit(solution)/shard_map/forward_stage/pallas_call | solution.py:565
  70.0 1.0 broadcast_in_dim.26.alpha
  71.0 28.5 %slope_stage.1.gsrc = bf16[4,16,16,384]{3,2,1,0:T(8,128)(2,1)} custom-call(bf16[4,16,16,384]{3,2,1,0:T(8,128)(2,1)} %forward_stage.1.src, f32[1024,128]{1,0:T(8,128)} %broadcast_in_dim.26.alpha, bf16[1024,1440]{1,0:T(8,128)(2,1)} %get-tuple-element.15.table, bf16[1440,1024]{1,0:T(8,128)(2,1)} %get-tuple-element.16.ttable, bf16[3,1440,128]{2,1,0:T(8,128)(2,1)} %upstream.3), custom_call_target="tpu_custom_call" | custom-call | tf_op jit(solution)/shard_map/slope_stage/pallas_call | solution.py:575
  99.5 43.3 %backward_stage.1 = (bf16[4,16,16,384]{3,2,1,0:T(8,128)(2,1)}, f32[16,48,128]{2,1,0:T(8,128)}) custom-call(bf16[4,16,16,384]{3,2,1,0:T(8,128)(2,1)} %get-tuple-element.12.src, bf16[4,16,16,384]{3,2,1,0:T(8,128)(2,1)} %slope_stage.1.gsrc, bf16[16,512,128]{2,1,0:T(8,128)(2,1)} %get-tuple-element.13.anal, bf16[16,512,128]{2,1,0:T(8,128)(2,1)} %get-tuple-element.17.synth, ...), custom_call_target="tpu_custom_call" | custom-call | tf_op jit(solution)/shard_map/backward_stage/pallas_call | solution.py:591
  142.8 0.0 copy-start
  142.8 5.8 %final_stage.1 = bf16[3,1440,128]{2,1,0:T(8,128)(2,1)} custom-call(bf16[4,16,16,384]{3,2,1,0:T(8,128)(2,1)} %get-tuple-element.19.src, bf16[1440,1024]{1,0:T(8,128)(2,1)} %get-tuple-element.16.ttable, bf16[3,1440,128]{2,1,0:T(8,128)(2,1)} %upstream.3), custom_call_target="tpu_custom_call" | custom-call | tf_op jit(solution)/shard_map/final_stage/pallas_call | solution.py:612
  148.7 0.0 copy-done
  148.7 0.7 slice.55
  149.4 0.7 slice.54
  (10 shorter events, 0.0 us)
Async XLA Ops:
  5.7 37.5 %copy-start.1 = (bf16[2,128,128]{2,1,0:T(8,128)(2,1)S(1)}, bf16[2,128,128]{2,1,0:T(8,128)(2,1)}, u32[]{:S(2)}) copy-start(bf16[2,128,128]{2,1,0:T(8,128)(2,1)} %param.6) | copy-start | bytes 196612
  142.8 5.8 %copy-start = (f32[16,48,128]{2,1,0:T(8,128)S(1)}, f32[16,48,128]{2,1,0:T(8,128)}, u32[]{:S(2)}) copy-start(f32[16,48,128]{2,1,0:T(8,128)} %get-tuple-element.20) | copy-start | bytes 1179652

commit v3 on v2

v3 whole, which is shorter than its diff:
```python
import functools
import math

import jax
import jax.numpy as jnp
import numpy as np
from jax import lax
from jax.experimental import pallas as pl
from jax.experimental.pallas import tpu as pltpu
from jax.sharding import PartitionSpec as P

MODES = 512
ROWS = 32
F32 = jnp.float32
BF16 = jnp.bfloat16


def params(**extra):
    return pltpu.CompilerParams(vmem_limit_bytes=56 * 1024 * 1024, **extra)


def latitude_angles(index, lat_count):
    return math.pi * (index.astype(F32) + 0.5) / lat_count


def greet(devices):
    me = lax.axis_index("space")
    barrier = pltpu.get_barrier_semaphore()

    def hello(step, carry):
        peer = (me + step) % devices
        pl.semaphore_signal(
            barrier, inc=1, device_id={"space": peer}, device_id_type=pl.DeviceIdType.MESH
        )
        return carry

    lax.fori_loop(1, devices, hello, 0)


def await_greetings(devices):
    pl.semaphore_wait(pltpu.get_barrier_semaphore(), devices - 1)


def remote(src, dst, send_sem, recv_sem, peer):
    return pltpu.make_async_remote_copy(
        src_ref=src,
        dst_ref=dst,
        send_sem=send_sem,
        recv_sem=recv_sem,
        device_id={"space": peer},
        device_id_type=pl.DeviceIdType.MESH,
    )


class Exchange:
    def __init__(self, source, target, send_sem, recv_sem):
        self.source, self.target = source, target
        self.send_sem, self.recv_sem = send_sem, recv_sem
        self.devices = source.shape[1]
        self.me = lax.axis_index("space")

    def copy(self, section, step):
        peer = (self.me + step) % self.devices
        return remote(
            self.source.at[section, peer],
            self.target.at[section, self.me],
            self.send_sem.at[section, step],
            self.recv_sem.at[section, step],
            peer,
        )

    def send(self, section):
        half = self.devices // 2

        def one(index, carry):
            sign = 1 - 2 * (index % 2)
            step = (half + sign * ((index + 1) // 2) + self.devices) % self.devices
            self.copy(section, step).start()
            return carry

        lax.fori_loop(0, self.devices - 1, one, 0)
        self.target[section, self.me] = self.source[section, self.me]

    def arrive(self, section):
        def one(step, carry):
            self.copy(section, step).wait_recv()
            return carry

        lax.fori_loop(1, self.devices, one, 0)

    def drain(self):
        for section in range(self.source.shape[0]):

            def one(step, carry, section=section):
                self.copy(section, step).wait_send()
                return carry

            lax.fori_loop(1, self.devices, one, 0)


class Reduction:
    def __init__(self, red, inbox, total, send_sem, recv_sem):
        self.red, self.inbox, self.total = red, inbox, total
        self.send_sem, self.recv_sem = send_sem, recv_sem
        devices = red.shape[0]
        me = lax.axis_index("space")
        self.hops = []
        base = me * 0
        stride = 1
        while stride < devices:
            half = devices // (2 * stride)
            bit = me // stride % 2
            keep, give = base + bit * half, base + (1 - bit) * half
            self.hops.append((half, keep, give, me + (1 - 2 * bit) * stride))
            base = keep
            stride *= 2
        self.base = base

    def scatter(self):
        for t, (half, keep, give, partner) in enumerate(self.hops):
            copy = remote(
                self.red.at[pl.ds(give, half)],
                self.inbox.at[pl.ds(half, half)],
                self.send_sem.at[t],
                self.recv_sem.at[t],
                partner,
            )
            copy.start()
            copy.wait()
            self.red[pl.ds(keep, half)] += self.inbox[half : 2 * half]
        self.total[pl.ds(self.base, 1)] = self.red[pl.ds(self.base, 1)]

    def gather(self, index):
        count = len(self.hops)
        t = count - 1 - index
        half, keep, _, partner = self.hops[t]
        block = self.total.at[pl.ds(keep, half)]
        copy = remote(
            block, block, self.send_sem.at[count + t], self.recv_sem.at[count + t], partner
        )
        copy.start()
        return copy


def sections_of(devices):
    return max(1, min(4, MODES // devices // 8))


def row_phase(rows, devices, lon_count):
    span = 2 * MODES // devices // sections_of(devices)
    section = rows // (span * devices)
    device = rows // span % devices
    part = rows // (span // 2) % 2
    slot = section * (span // 2) + rows % (span // 2)
    return slot * devices + device, part * (lon_count // 4)


def cosine_of(phase, lon_count):
    turn = phase - jnp.floor(phase * (1.0 / lon_count)) * lon_count
    x = (lon_count / 4 - jnp.abs(turn - lon_count / 2)) * (2.0 * math.pi / lon_count)
    y = x * x
    tail = 1.0 / 362880.0 - y * (1.0 / 39916800.0)
    tail = 1.0 / 120.0 + y * (-1.0 / 5040.0 + y * tail)
    return -x * (1.0 + y * (-1.0 / 6.0 + y * tail))


def angle_indices(devices, lon_count):
    order, offset = row_phase(np.arange(2 * MODES), devices, lon_count)

    def column(values):
        return np.broadcast_to(values.astype(np.float32)[:, None], (len(values), 128))

    def lanes(values):
        return np.broadcast_to(values.astype(np.float32)[None, :], (8, len(values)))

    columns = np.stack([column(v) for v in (order[::ROWS], offset[::ROWS], order[:ROWS], offset[:ROWS])])
    return jnp.asarray(columns), jnp.asarray(np.stack([lanes(order), lanes(offset)]))


def angles_by_row(columns, lon_count, big, small):
    rows = big.shape[1]
    lon = lax.broadcasted_iota(jnp.int32, (rows, lon_count), 1).astype(F32)
    phase = columns[0][:, 0:1] * lon + columns[1][:, 0:1]
    big[0] = cosine_of(phase, lon_count)
    big[1] = cosine_of(phase + 0.75 * lon_count, lon_count)
    lon = lax.broadcasted_iota(jnp.int32, (ROWS, lon_count), 1).astype(F32)
    phase = columns[2][:, 0:1] * lon + columns[3][:, 0:1]
    factor = 1.0 / math.sqrt(lon_count)
    small[0] = cosine_of(phase, lon_count) * factor
    small[1] = cosine_of(phase + 0.75 * lon_count, lon_count) * factor


def angles_by_lane(lanes, lon_count, big, small):
    rows, total = big.shape[1:]
    order, offset = lanes[0, 0:1, :], lanes[1, 0:1, :]
    lon = lax.broadcasted_iota(jnp.int32, (rows, total), 0).astype(F32) * float(ROWS)
    phase = lon * order
    big[0] = cosine_of(phase, lon_count)
    big[1] = cosine_of(phase + 0.75 * lon_count, lon_count)
    lon = lax.broadcasted_iota(jnp.int32, (ROWS, total), 0).astype(F32)
    phase = lon * order + offset
    factor = 1.0 / math.sqrt(lon_count)
    small[0] = cosine_of(phase, lon_count) * factor
    small[1] = cosine_of(phase + 0.75 * lon_count, lon_count) * factor


def fill(dst, big, small, count):
    def step(h, carry):
        value = big[0, pl.ds(h, 1), :] * small[0] - big[1, pl.ds(h, 1), :] * small[1]
        dst[pl.ds(pl.multiple_of(h * ROWS, ROWS), ROWS), :] = value.astype(BF16)
        return carry

    lax.fori_loop(0, count, step, 0)


def alpha_column(section, rows, span):
    row = lax.broadcasted_iota(jnp.int32, (rows, 128), 0)
    zero = jnp.logical_or(row == 0, row == span // 2)
    alpha = jnp.where(zero, 1.0, 2.0) if section == 0 else jnp.full((rows, 128), 2.0, F32)
    return alpha[:, 0:1]


def section_product(table, wide, out, section, scaled):
    _, devices, span, width = out.shape
    count = devices * span
    chunk = 256
    each = chunk // span
    for q in range(count // chunk):
        first = section * count + q * chunk
        value = jnp.dot(table[first : first + chunk, :], wide, preferred_element_type=F32)
        if scaled:
            value = value * (alpha_column(0, chunk, span) if first == 0 else 2.0)
        out[section, q * each : (q + 1) * each] = value.astype(BF16).reshape(each, span, width)


def legendre_tables(
    slot_ref, start_ref, lat_ref, synth, anal, tsynth, tanal, hold
):
    groups, width = slot_ref.shape
    orders = slot_ref[...] + lax.axis_index("space").astype(F32)
    order_sq = orders * orders
    cosine = lat_ref[0:1, :]
    wrow = lat_ref[1:2, :]
    wcol = jnp.broadcast_to(wrow, (128, width)).T[:, 0:1]
    block = 32

    def degree_block(index, carry):
        p_now, p_prev, e_prev, log_scale = carry
        scale = jnp.exp(log_scale)
        base = index * block
        for inner in range(block):
            degree_int = base + inner
            degree = degree_int.astype(F32)
            active = degree > orders
            square = degree * degree
            ratio = jnp.maximum(square - order_sq, 1.0) / jnp.maximum(4.0 * square - 1.0, 1.0)
            coef = lax.rsqrt(ratio)
            p_next = jnp.where(active, coef * (cosine * p_now - e_prev * p_prev), p_now)
            p_prev = jnp.where(active, p_now, p_prev)
            e_prev = jnp.where(active, ratio * coef, 0.0)
            p_now = p_next
            value = jnp.where(degree >= orders, p_now * scale, 0.0)
            rows = pl.ds(pl.multiple_of(degree_int * groups, groups), groups)
            for part in range(width // 128):
                hold[part, rows, :] = value[:, part * 128 : (part + 1) * 128]
        magnitude = jnp.maximum(jnp.abs(p_now), jnp.abs(p_prev))
        return (p_now / magnitude, p_prev / magnitude, e_prev, log_scale + jnp.log(magnitude))

    ones = jnp.ones((groups, width), F32)
    zeros = jnp.zeros((groups, width), F32)
    lax.fori_loop(0, MODES // block, degree_block, (ones, zeros, zeros, start_ref[...]))

    def spread(g, carry):
        pieces = [
            hold[part, pl.ds(g, MODES, stride=groups), :]
            for part in range(width // 128)
        ]
        value = pieces[0] if len(pieces) == 1 else jnp.concatenate(pieces, 1)
        synth[g] = value.astype(BF16)
        anal[g] = (value * wrow).astype(BF16)
        turned = value.T
        tsynth[g] = turned.astype(BF16)
        tanal[g] = (turned * wcol).astype(BF16)
        return carry

    lax.fori_loop(0, synth.shape[0], spread, 0)


def unpack(src, scratch, q):
    _, devices, span, _ = src.shape
    for a in range(scratch.shape[0]):
        part = src[q, :, :, a * 128 : (a + 1) * 128].astype(F32)
        scratch[a, q * devices * span : (q + 1) * devices * span] = part.reshape(devices * span, 128)


def pack(scratch, dst, q):
    _, devices, span, _ = dst.shape
    for a in range(scratch.shape[0]):
        part = scratch[a, q * devices * span : (q + 1) * devices * span]
        dst[q, :, :, a * 128 : (a + 1) * 128] = part.reshape(devices, span, 128).astype(BF16)


def strided_rows(s, r, devices, span):
    half = span // 2
    start = s // half * (devices * span) + r * half + s % half
    return pl.ds(start, devices, stride=span)


def gather_group(scratch, g, devices, span, per_group, height):
    lat_local = scratch.shape[0]
    rows = []
    for j in range(per_group):
        s = g * per_group + j
        halves = []
        for r in range(2):
            pick = strided_rows(s, r, devices, span)
            parts = [scratch[a, pick, :] for a in range(lat_local)]
            if height > devices * lat_local:
                parts.append(jnp.zeros((height - devices * lat_local, 128), F32))
            halves.append(jnp.concatenate(parts, 0))
        zero = jnp.zeros((height, 256), F32)
        cells = [zero] * per_group
        cells[j] = jnp.concatenate(halves, 1)
        rows.append(cells[0] if per_group == 1 else jnp.concatenate(cells, 1))
    return (rows[0] if per_group == 1 else jnp.concatenate(rows, 0)).astype(BF16)


def scatter_group(value, scratch, g, devices, span, per_group, height):
    lat_local = scratch.shape[0]
    for j in range(per_group):
        s = g * per_group + j
        for r in range(2):
            for a in range(lat_local):
                top = j * height + a * devices
                left = j * 256 + r * 128
                scratch[a, strided_rows(s, r, devices, span), :] = value[
                    top : top + devices, left : left + 128
                ]


def over_groups(groups, sections, section, body):
    pieces = 4
    each = groups // pieces
    share = pieces // sections
    for q in range(section * share, (section + 1) * share):
        first = q * (MODES // pieces)
        lax.fori_loop(q * each, (q + 1) * each, functools.partial(body, first), 0)


def widen(filter_ref, first, copies):
    gain = filter_ref[first:, :].astype(F32)
    return jnp.concatenate([gain] * copies, 1)


def forward_body(per_group, shapes, anal, tsynth, filt, weight, scratch, back):
    _, devices, span, _ = shapes
    height = anal.shape[2] // per_group

    def body(first, g, carry):
        operand = gather_group(scratch, g, devices, span, per_group, height)
        spectrum = jnp.dot(anal[g, first:, :], operand, preferred_element_type=F32).astype(BF16)
        scaled = (spectrum.astype(F32) * widen(filt, first, 2 * per_group)).astype(BF16)
        mixed = [
            jnp.dot(
                scaled[:, j * 256 : (j + 1) * 256], weight[...], preferred_element_type=F32
            ).astype(BF16)
            for j in range(per_group)
        ]
        mixed = mixed[0] if per_group == 1 else jnp.concatenate(mixed, 1)
        value = jnp.dot(tsynth[g, :, first:], mixed, preferred_element_type=F32)
        scatter_group(value, back, g, devices, span, per_group, height)
        return carry

    return body


def backward_body(
    per_group, shapes, anal, synth, tanal, filt, weight, scratch, gscratch, wgrad, fgrad
):
    _, devices, span, _ = shapes
    height = anal.shape[2] // per_group

    def body(first, g, carry):
        operand = gather_group(scratch, g, devices, span, per_group, height)
        goperand = gather_group(gscratch, g, devices, span, per_group, height)
        gain = widen(filt, first, 2)
        outs = []
        spectrum = jnp.dot(anal[g, first:, :], operand, preferred_element_type=F32).astype(BF16)
        gmixed = jnp.dot(synth[g, first:, :], goperand, preferred_element_type=F32).astype(BF16)
        for j in range(per_group):
            lanes = slice(j * 256, (j + 1) * 256)
            spec = spectrum[:, lanes].astype(F32)
            scaled = (spec * gain).astype(BF16)
            gmix = gmixed[:, lanes]
            wgrad[...] += lax.dot_general(
                scaled, gmix, (((0,), (0,)), ((), ())), preferred_element_type=F32
            )
            gscaled = lax.dot_general(
                gmix, weight[...], (((1,), (1,)), ((), ())), preferred_element_type=F32
            )
            term = gscaled * spec
            fgrad[first:, :] += term[:, :128] + term[:, 128:]
            outs.append((gscaled * gain).astype(BF16))
        gspectrum = outs[0] if per_group == 1 else jnp.concatenate(outs, 1)
        value = jnp.dot(tanal[g, :, first:], gspectrum, preferred_element_type=F32)
        scatter_group(value, scratch, g, devices, span, per_group, height)
        return carry

    return body


def fold_gradients(wgrad, fgrad, red):
    half = wgrad.shape[0] // 2
    pieces = [
        (wgrad[:half, :half] + wgrad[half:, half:]) * (1.0 / MODES),
        (wgrad[:half, half:] - wgrad[half:, :half]) * (1.0 / MODES),
        fgrad[...] * 0.125,
    ]
    spare = red.shape[0] * red.shape[1] - 2 * half - MODES
    if spare:
        pieces.append(jnp.zeros((spare, 128), F32))
    red[...] = jnp.concatenate(pieces, 0).reshape(red.shape)


def gelu_slope(field):
    return 0.5 * (1.0 + lax.erf(field * (1.0 / math.sqrt(2.0)))) + field * jnp.exp(
        -0.5 * field * field
    ) * (1.0 / math.sqrt(2.0 * math.pi))


LON_CHUNK = 288


def merged(src, section):
    _, devices, span, width = src.shape
    return src[section].astype(F32).reshape(devices * span, width)


def add_section(ttable, operand, section, field, last):
    count = operand.shape[0]
    lon_count = field.shape[0]

    def grid_rows(q, carry):
        rows = pl.ds(pl.multiple_of(q * LON_CHUNK, LON_CHUNK), LON_CHUNK)
        value = jnp.dot(
            ttable[rows, section * count : (section + 1) * count],
            operand,
            preferred_element_type=F32,
        )
        if section:
            value = value + field[rows, :]
        if last is None:
            field[rows, :] = value
        else:
            last(rows, value)
        return carry

    lax.fori_loop(0, lon_count // LON_CHUNK, grid_rows, 0)


def block_kernel(
    per_group,
    columns, lanes, grid, upstream, slots, start, lats, filt, weight,
    grad, total,
    table, ttable, big, small, tbig, tsmall,
    synth, anal, tsynth, tanal, hold,
    out1, in1, out2, in2, out3, in3, out4, in4,
    scratch, back, field, slope, wgrad, fgrad, red, inbox,
    send1, recv1, send2, recv2, send3, recv3, send4, recv4, rsend, rrecv,
):
    shapes = out1.shape
    sections, devices, span, _ = shapes
    lat_local, lon_count, channels = grid.shape
    groups = synth.shape[0]
    greet(devices)
    angles_by_row(columns, lon_count, big, small)
    fill(table, big, small, big.shape[1])

    first = Exchange(out1, in1, send1, recv1)
    wide = jnp.concatenate([grid[a] for a in range(lat_local)], 1)
    for q in range(sections):
        section_product(table, wide, out1, q, False)
        if q == 0:
            await_greetings(devices)
        first.send(q)
    legendre_tables(slots, start, lats, synth, anal, tsynth, tanal, hold)
    angles_by_lane(lanes, lon_count, tbig, tsmall)
    fill(ttable, tbig, tsmall, tbig.shape[1])

    second = Exchange(out2, in2, send2, recv2)
    forward = forward_body(per_group, shapes, anal, tsynth, filt, weight, scratch, back)
    for q in range(sections):
        first.arrive(q)
        unpack(in1, scratch, q)
        over_groups(groups, sections, q, forward)
        pack(back, out2, q)
        second.send(q)

    def gate(rows, value):
        up = jnp.concatenate([upstream[a, rows, :] for a in range(lat_local)], 1)
        slope[rows, :] = (up.astype(F32) * gelu_slope(value)).astype(BF16)

    for q in range(sections):
        second.arrive(q)
        operand = merged(in2, q)
        operand = (operand * alpha_column(q, operand.shape[0], span)).astype(BF16)
        add_section(ttable, operand, q, field, gate if q == sections - 1 else None)

    third = Exchange(out3, in3, send3, recv3)
    for q in range(sections):
        section_product(table, slope[...], out3, q, True)
        third.send(q)

    wgrad[...] = jnp.zeros_like(wgrad)
    fgrad[...] = jnp.zeros_like(fgrad)
    fourth = Exchange(out4, in4, send4, recv4)
    backward = backward_body(
        per_group, shapes, anal, synth, tanal, filt, weight, scratch, back, wgrad, fgrad
    )
    for q in range(sections):
        third.arrive(q)
        unpack(in3, back, q)
        over_groups(groups, sections, q, backward)
        pack(scratch, out4, q)
        if q < sections - 1:
            fourth.send(q)
    fold_gradients(wgrad, fgrad, red)
    reduction = Reduction(red, inbox, total, rsend, rrecv)
    reduction.scatter()
    fourth.send(sections - 1)

    def finish(rows, value):
        for a in range(lat_local):
            part = value[:, a * channels : (a + 1) * channels]
            grad[a, rows, :] = (part + upstream[a, rows, :].astype(F32)).astype(BF16)

    hops = len(reduction.hops)
    for step in range(max(hops, sections)):
        copy = reduction.gather(step) if step < hops else None
        if step < sections:
            fourth.arrive(step)
            add_section(
                ttable,
                merged(in4, step).astype(BF16),
                step,
                field,
                finish if step == sections - 1 else None,
            )
        if copy is not None:
            copy.wait()
    for exchange in (first, second, third, fourth):
        exchange.drain()


def mixing_matrix(mix_weight):
    upper = jnp.concatenate([mix_weight[0], mix_weight[1]], 1)
    lower = jnp.concatenate([-mix_weight[1], mix_weight[0]], 1)
    return jnp.concatenate([upper, lower], 0)


def body(grid_in, upstream, mix_weight, degree_filter):
    devices = lax.axis_size("space")
    me = lax.axis_index("space")
    lat_local, lon_count, channels = grid_in.shape
    lat_count = lat_local * devices
    slots = MODES // devices
    sections = sections_of(devices)
    span = 2 * slots // sections
    height = 64 if lat_count <= 64 else -(-lat_count // 128) * 128
    per_group = 128 // height if height < 128 else 1
    width = height * per_group
    groups = slots // per_group
    dims = (sections, devices, span, lat_local * channels)

    lane = np.arange(width)
    within = lane % height
    valid = within < lat_count
    latitude = np.where(valid, within % devices * lat_local + within // devices, 0)
    padded = -(-groups // 8) * 8
    group = np.minimum(np.arange(padded), groups - 1)[:, None]
    slot_orders = ((group * per_group + lane[None, :] // height) * devices).astype(np.float32)
    slot_orders = jnp.asarray(slot_orders)
    angles = latitude_angles(jnp.asarray(latitude), lat_count)
    orders = slot_orders + me.astype(F32)
    start = 0.5 * (jnp.log(2.0 * orders + 1.0) - math.log(2.0))
    start = start + 0.5 * (
        lax.lgamma(2.0 * orders + 1.0) - 2.0 * lax.lgamma(orders + 1.0) - orders * math.log(4.0)
    )
    start = start + orders * jnp.log(jnp.sin(angles))[None, :]
    row = jnp.arange(8)[:, None]
    weights = math.pi / lat_count * jnp.sin(angles) * jnp.asarray(valid.astype(np.float32))
    lats = jnp.where(row == 0, jnp.cos(angles)[None, :], weights[None, :])

    share = -(-(2 * channels + MODES) // (8 * devices)) * 8
    blocks = (devices, share, channels)
    vmem = pltpu.VMEM
    slab = vmem((lat_local, 2 * MODES, 128), F32)
    total_rows = 2 * MODES
    semaphores = pltpu.SemaphoreType.DMA((sections, devices))
    hops = pltpu.SemaphoreType.DMA((2 * devices.bit_length(),))
    grad_in, summed = pl.pallas_call(
        functools.partial(block_kernel, per_group),
        out_shape=(
            jax.ShapeDtypeStruct(grid_in.shape, BF16),
            jax.ShapeDtypeStruct(blocks, F32),
        ),
        scratch_shapes=[
            vmem((total_rows, lon_count), BF16),
            vmem((lon_count, total_rows), BF16),
            vmem((2, total_rows // ROWS, lon_count), F32),
            vmem((2, ROWS, lon_count), F32),
            vmem((2, lon_count // ROWS, total_rows), F32),
            vmem((2, ROWS, total_rows), F32),
            vmem((groups, MODES, width), BF16),
            vmem((groups, MODES, width), BF16),
            vmem((groups, width, MODES), BF16),
            vmem((groups, width, MODES), BF16),
            vmem((width // 128, MODES * padded, 128), F32),
            *[vmem(dims, BF16)] * 8,
            slab,
            slab,
            vmem((lon_count, lat_local * channels), F32),
            vmem((lon_count, lat_local * channels), BF16),
            vmem((2 * channels, 2 * channels), F32),
            vmem((MODES, channels), F32),
            vmem(blocks, F32),
            vmem(blocks, F32),
            *[semaphores] * 8,
            hops,
            hops,
        ],
        compiler_params=params(collective_id=0, has_side_effects=True),
        name="block",
    )(
        *angle_indices(devices, lon_count),
        grid_in,
        upstream,
        slot_orders,
        start,
        lats,
        degree_filter,
        mixing_matrix(mix_weight),
    )
    summed = summed.reshape(devices * share, channels)
    return (
        grad_in,
        summed[: 2 * channels].reshape(2, channels, channels),
        summed[2 * channels : 2 * channels + MODES],
    )


def solution(mesh):
    return jax.shard_map(
        body,
        mesh=mesh,
        in_specs=(P(("groups", "space"), None, None), P(("groups", "space"), None, None), P(), P()),
        out_specs=(P(("groups", "space"), None, None), P("groups", None, None), P("groups", None)),
        check_vma=False,
    )
```

time: 150 us -> 115 us (0.77)
  Pallas kernels: 136 us -> 104 us
  other arithmetic: 8.75 us -> 4.2 us
  local copies, waits for them, and re-layouts: 4.67 us -> 6.32 us
    pallas_call x5 -> x1, Pallas kernels: 136 us -> 104 us  [body(): pl.pallas_call(functools.partial(block_kernel, per_group), out_shape=(jax...]
    cos x5 -> x0, other arithmetic: 3.39 us -> none  [the longest x4 3.34 us: trig(): return jnp.stack([jnp.cos(angles), jnp.sin(angles)], 0)]
    broadcast_in_dim x4 -> x0, local copies, waits for them, and re-layouts: 2.9 us -> none  [the longest x1 0.99 us: body(): jnp.broadcast_to(jnp.where(order == 0, 1.0, 2.0).astype(F32)[:, None], (2...]
    unnamed x4 -> x1, local copies, waits for them, and re-layouts: 0.01 us -> 2.3 us
    another operation x2 -> x0, other arithmetic: 1.55 us -> none  [trig(): return jnp.stack([jnp.cos(angles), jnp.sin(angles)], 0)]
    mul x3 -> x0, other arithmetic: 1.54 us -> none  [the longest x1 0.81 us: base_tables(): trig(fine, lon_count) * factor]
where the time goes in v3:
time: 115 us
  Pallas kernels  104 us (90%)
  local copies, waits for them, and re-layouts  6.32 us (5%)
  other arithmetic  4.2 us (4%)
    pallas_call x1, Pallas kernels, body(): pl.pallas_call(functools.partial(block_kernel, per_group), out_shape=(jax...  104 us
    unnamed x1, local copies, waits for them, and re-layouts  2.3 us

profile of v3, /device:TPU:0, one launch (start us, length us, event | category | flops | bytes accessed | tf_op | source)
XLA Modules:
  0.0 114.9 jit_solution(10747991889791446371)
XLA Ops:
  0.6 1.3 %broadcast_select_fusion.lats = f32[8,128]{1,0:T(8,128)} fusion(f32[128]{0:T(128)} %constant.95, f32[128]{0:T(128)} %constant.93, pred[8]{0:T(512)(128)(4,1)S(1)} %iota_compare_fusion), kind=kLoop, calls=%fused_computation.79 | loop fusion | flops 1024 | bytes 5128 | tf_op jit(solution)/shard_map/jit(_where)/select_n | solution.py:592
  2.0 1.4 %fusion.16.start = f32[16,128]{1,0:T(8,128)} fusion(f32[16,128]{1,0:T(8,128)} %constant.81.clone.slots, f32[128]{0:T(128)} %constant.92, f32[]{:T(128)S(6)} %convert_element_type.6), kind=kLoop, calls=%fused_computation.27 | loop fusion | flops 235520 | bytes 16900 | tf_op jit(solution)/shard_map/add | solution.py:589
  3.4 0.8 fusion.68
  4.2 0.8 slice_bitcast_fusion
  5.0 0.7 maximum_maximum_fusion.weight
  5.6 103.8 %block.1 = (bf16[3,1440,128]{2,1,0:T(8,128)(2,1)}, f32[16,48,128]{2,1,0:T(8,128)}) custom-call(f32[4,32,128]{2,1,0:T(8,128)} %constant.84.clone.columns, f32[2,8,1024]{2,1,0:T(8,128)} %constant.85.clone.lanes, bf16[3,1440,128]{2,1,0:T(8,128)(2,1)} %grid.1, bf16[3,1440,128]{2,1,0:T(8,128)(2,1)} %upstream.1, f32[16,128]{1,0:T(8,128)} %constant.81.clone.slots, ...), custom_call_target="tpu_custom_call" | custom-call | tf_op jit(solution)/shard_map/block/pallas_call | solution.py:601
  109.4 1.6 %slice.18 = f32[256,128]{1,0:T(8,128)} slice(f32[768,128]{1,0:T(8,128)} %bitcast.8), slice={[0:256], [0:128]} | slice | bytes 262144 | tf_op jit(solution)/shard_map/slice | solution.py:647
  110.9 1.7 %slice.19 = f32[512,128]{1,0:T(8,128)} slice(f32[768,128]{1,0:T(8,128)} %bitcast.9), slice={[256:768], [0:128]} | slice | bytes 524288 | tf_op jit(solution)/shard_map/slice | solution.py:648
  112.6 2.3 %copy.13 = bf16[3,1440,128]{2,1,0:T(8,128)(2,1)} copy(bf16[3,1440,128]{2,1,0:T(8,128)(2,1)} %get-tuple-element.12) | data formatting | bytes 2211840
  (1 shorter events, 0.0 us)

commit v4 on v3

--- a/solution.py
+++ b/solution.py
@@ -116,7 +116,12 @@
             stride *= 2
         self.base = base
 
-    def scatter(self):
+    def scatter(self, held):
+        count = len(self.hops)
+        early = max(1, len(held) - 2) if held else 0
+        for send in held[:early]:
+            send()
+        late = held[early:]
         for t, (half, keep, give, partner) in enumerate(self.hops):
             copy = remote(
                 self.red.at[pl.ds(give, half)],
@@ -126,6 +131,9 @@
                 partner,
             )
             copy.start()
+            index = t - (count - len(late))
+            if index >= 0:
+                late[index]()
             copy.wait()
             self.red[pl.ds(keep, half)] += self.inbox[half : 2 * half]
         self.total[pl.ds(self.base, 1)] = self.red[pl.ds(self.base, 1)]
@@ -460,9 +468,9 @@
 
 def block_kernel(
     per_group,
-    columns, lanes, grid, upstream, slots, start, lats, filt, weight,
-    grad, total,
-    table, ttable, big, small, tbig, tsmall,
+    columns, lanes, grid, upstream, slots, start, lats, filt, mix_weight,
+    grad, grad_weight, grad_filter,
+    weight, total, table, ttable, big, small, tbig, tsmall,
     synth, anal, tsynth, tanal, hold,
     out1, in1, out2, in2, out3, in3, out4, in4,
     scratch, back, field, slope, wgrad, fgrad, red, inbox,
@@ -473,6 +481,10 @@
     lat_local, lon_count, channels = grid.shape
     groups = synth.shape[0]
     greet(devices)
+    weight[:channels, :channels] = mix_weight[0]
+    weight[:channels, channels:] = mix_weight[1]
+    weight[channels:, :channels] = -mix_weight[1]
+    weight[channels:, channels:] = mix_weight[0]
     angles_by_row(columns, lon_count, big, small)
     fill(table, big, small, big.shape[1])
 
@@ -522,12 +534,11 @@
         unpack(in3, back, q)
         over_groups(groups, sections, q, backward)
         pack(scratch, out4, q)
-        if q < sections - 1:
+        if q == 0:
             fourth.send(q)
     fold_gradients(wgrad, fgrad, red)
     reduction = Reduction(red, inbox, total, rsend, rrecv)
-    reduction.scatter()
-    fourth.send(sections - 1)
+    reduction.scatter([functools.partial(fourth.send, q) for q in range(1, sections)])
 
     def finish(rows, value):
         for a in range(lat_local):
@@ -548,14 +559,12 @@
             )
         if copy is not None:
             copy.wait()
+    sums = total[...].reshape(-1, channels)
+    for r in range(2):
+        grad_weight[r] = sums[r * channels : (r + 1) * channels]
+    grad_filter[...] = sums[2 * channels : 2 * channels + MODES]
     for exchange in (first, second, third, fourth):
         exchange.drain()
-
-
-def mixing_matrix(mix_weight):
-    upper = jnp.concatenate([mix_weight[0], mix_weight[1]], 1)
-    lower = jnp.concatenate([-mix_weight[1], mix_weight[0]], 1)
-    return jnp.concatenate([upper, lower], 0)
 
 
 def body(grid_in, upstream, mix_weight, degree_filter):
@@ -598,13 +607,16 @@
     total_rows = 2 * MODES
     semaphores = pltpu.SemaphoreType.DMA((sections, devices))
     hops = pltpu.SemaphoreType.DMA((2 * devices.bit_length(),))
-    grad_in, summed = pl.pallas_call(
+    return pl.pallas_call(
         functools.partial(block_kernel, per_group),
         out_shape=(
             jax.ShapeDtypeStruct(grid_in.shape, BF16),
-            jax.ShapeDtypeStruct(blocks, F32),
+            jax.ShapeDtypeStruct(mix_weight.shape, F32),
+            jax.ShapeDtypeStruct(degree_filter.shape, F32),
         ),
         scratch_shapes=[
+            vmem((2 * channels, 2 * channels), BF16),
+            vmem(blocks, F32),
             vmem((total_rows, lon_count), BF16),
             vmem((lon_count, total_rows), BF16),
             vmem((2, total_rows // ROWS, lon_count), F32),
@@ -639,13 +651,7 @@
         start,
         lats,
         degree_filter,
-        mixing_matrix(mix_weight),
-    )
-    summed = summed.reshape(devices * share, channels)
-    return (
-        grad_in,
-        summed[: 2 * channels].reshape(2, channels, channels),
-        summed[2 * channels : 2 * channels + MODES],
+        mix_weight,
     )
 
 

time: 115 us -> 112 us (0.974)
  local copies, waits for them, and re-layouts: 6.32 us -> 3.72 us
  other arithmetic: 4.2 us -> 2.77 us
    slice x2 -> x0, local copies, waits for them, and re-layouts: 3.24 us -> none  [the longest x1 1.67 us: body(): summed[2 * channels:2 * channels + MODES]]
    unnamed x1 -> x7, local copies, waits for them, and re-layouts: 2.3 us -> 3.72 us
where the time goes in v4:
time: 112 us
  Pallas kernels  104 us (93%)
  local copies, waits for them, and re-layouts  3.72 us (3%)
  other arithmetic  2.77 us (2%)
    pallas_call x1, Pallas kernels, body(): pl.pallas_call(functools.partial(block_kernel, per_group), out_shape=(jax...  104 us
    unnamed x7, local copies, waits for them, and re-layouts  3.72 us

profile of v4, /device:TPU:0, one launch (start us, length us, event | category | flops | bytes accessed | tf_op | source)
XLA Modules:
  0.0 111.5 jit_solution(2597503864714695471)
XLA Ops:
  0.6 1.3 %broadcast_select_fusion.lats = f32[8,128]{1,0:T(8,128)} fusion(f32[128]{0:T(128)} %constant.95, f32[128]{0:T(128)} %constant.93, pred[8]{0:T(512)(128)(4,1)S(1)} %iota_compare_fusion), kind=kLoop, calls=%fused_computation.76 | loop fusion | flops 1024 | bytes 5128 | tf_op jit(solution)/shard_map/jit(_where)/select_n | solution.py:601
  2.0 1.4 %fusion.16.start = f32[16,128]{1,0:T(8,128)} fusion(f32[16,128]{1,0:T(8,128)} %constant.81.clone.slots, f32[128]{0:T(128)} %constant.92, f32[]{:T(128)S(6)} %convert_element_type.6), kind=kLoop, calls=%fused_computation.24 | loop fusion | flops 235520 | bytes 16900 | tf_op jit(solution)/shard_map/add | solution.py:598
  3.4 104.4 %block.1 = (bf16[3,1440,128]{2,1,0:T(8,128)(2,1)}, f32[2,128,128]{2,1,0:T(8,128)}, f32[512,128]{1,0:T(8,128)}) custom-call(f32[4,32,128]{2,1,0:T(8,128)} %constant.84.clone.columns, f32[2,8,1024]{2,1,0:T(8,128)} %constant.85.clone.lanes, bf16[3,1440,128]{2,1,0:T(8,128)(2,1)} %grid.1, bf16[3,1440,128]{2,1,0:T(8,128)(2,1)} %upstream.1, ...), custom_call_target="tpu_custom_call" | custom-call | tf_op jit(solution)/shard_map/block/pallas_call | solution.py:610
  107.8 0.0 copy-start.1
  107.8 0.0 copy-start
  107.8 2.4 %copy.15 = bf16[3,1440,128]{2,1,0:T(8,128)(2,1)} copy(bf16[3,1440,128]{2,1,0:T(8,128)(2,1)} %get-tuple-element.6) | data formatting | bytes 2211840
  110.2 0.0 copy-done.1
  110.2 0.7 copy.16
  110.8 0.0 copy-done
  110.8 0.7 copy.17
  (1 shorter events, 0.0 us)
Async XLA Ops:
  107.8 2.4 %copy-start.1 = (f32[2,128,128]{2,1,0:T(8,128)S(1)}, f32[2,128,128]{2,1,0:T(8,128)}, u32[]{:S(2)}) copy-start(f32[2,128,128]{2,1,0:T(8,128)} %get-tuple-element.7) | copy-start | bytes 393220
  107.8 3.0 %copy-start = (f32[512,128]{1,0:T(8,128)S(1)}, f32[512,128]{1,0:T(8,128)}, u32[]{:S(2)}) copy-start(f32[512,128]{1,0:T(8,128)} %get-tuple-element.8) | copy-start | bytes 786436

commit v5 on v4

--- a/solution.py
+++ b/solution.py
@@ -352,7 +352,14 @@
     share = pieces // sections
     for q in range(section * share, (section + 1) * share):
         first = q * (MODES // pieces)
-        lax.fori_loop(q * each, (q + 1) * each, functools.partial(body, first), 0)
+        pair = 2 if each % 2 == 0 else 1
+
+        def step(index, carry, first=first, pair=pair, q=q):
+            for j in range(pair):
+                body(first, q * each + index * pair + j, carry)
+            return carry
+
+        lax.fori_loop(0, each // pair, step, 0)
 
 
 def widen(filter_ref, first, copies):

time: 112 us -> 112 us (level)
  no operation moved by 1% of the time
where the time goes in v5:
time: 112 us
  Pallas kernels  104 us (93%)
  local copies, waits for them, and re-layouts  3.72 us (3%)
  other arithmetic  2.77 us (2%)
    pallas_call x1, Pallas kernels, body(): pl.pallas_call(functools.partial(block_kernel, per_group), out_shape=(jax...  104 us
    unnamed x7, local copies, waits for them, and re-layouts  3.72 us

profile of v5, /device:TPU:0, one launch (start us, length us, event | category | flops | bytes accessed | tf_op | source)
XLA Modules:
  0.0 111.6 jit_solution(14095761732858077164)
XLA Ops:
  0.6 1.3 %broadcast_select_fusion.lats = f32[8,128]{1,0:T(8,128)} fusion(f32[128]{0:T(128)} %constant.95, f32[128]{0:T(128)} %constant.93, pred[8]{0:T(512)(128)(4,1)S(1)} %iota_compare_fusion), kind=kLoop, calls=%fused_computation.76 | loop fusion | flops 1024 | bytes 5128 | tf_op jit(solution)/shard_map/jit(_where)/select_n | solution.py:608
  2.0 1.4 %fusion.16.start = f32[16,128]{1,0:T(8,128)} fusion(f32[16,128]{1,0:T(8,128)} %constant.81.clone.slots, f32[128]{0:T(128)} %constant.92, f32[]{:T(128)S(6)} %convert_element_type.6), kind=kLoop, calls=%fused_computation.24 | loop fusion | flops 235520 | bytes 16900 | tf_op jit(solution)/shard_map/add | solution.py:605
  3.4 104.4 %block.1 = (bf16[3,1440,128]{2,1,0:T(8,128)(2,1)}, f32[2,128,128]{2,1,0:T(8,128)}, f32[512,128]{1,0:T(8,128)}) custom-call(f32[4,32,128]{2,1,0:T(8,128)} %constant.84.clone.columns, f32[2,8,1024]{2,1,0:T(8,128)} %constant.85.clone.lanes, bf16[3,1440,128]{2,1,0:T(8,128)(2,1)} %grid.1, bf16[3,1440,128]{2,1,0:T(8,128)(2,1)} %upstream.1, ...), custom_call_target="tpu_custom_call" | custom-call | tf_op jit(solution)/shard_map/block/pallas_call | solution.py:617
  107.8 0.0 copy-start.1
  107.8 0.0 copy-start
  107.8 2.4 %copy.15 = bf16[3,1440,128]{2,1,0:T(8,128)(2,1)} copy(bf16[3,1440,128]{2,1,0:T(8,128)(2,1)} %get-tuple-element.6) | data formatting | bytes 2211840
  110.2 0.0 copy-done.1
  110.2 0.7 copy.16
  110.9 0.0 copy-done
  110.9 0.7 copy.17
  (1 shorter events, 0.0 us)
Async XLA Ops:
  107.8 2.4 %copy-start.1 = (f32[2,128,128]{2,1,0:T(8,128)S(1)}, f32[2,128,128]{2,1,0:T(8,128)}, u32[]{:S(2)}) copy-start(f32[2,128,128]{2,1,0:T(8,128)} %get-tuple-element.7) | copy-start | bytes 393220
  107.8 3.0 %copy-start = (f32[512,128]{1,0:T(8,128)S(1)}, f32[512,128]{1,0:T(8,128)}, u32[]{:S(2)}) copy-start(f32[512,128]{1,0:T(8,128)} %get-tuple-element.8) | copy-start | bytes 786436
